TPU v7x, 32 devices: a whole 2x2x4 slice. The times are simulated.
32 devices in a mesh: section: 2 (over x), fsdp: 4 (over z), tp: 4 (over y, core).
Axes of the slice: x: 2, y: 2, z: 4, core: 2. Of those that a mesh axis runs over, the one named last changes fastest.
Arguments:
- inputs: bfloat16 [2, 1024, 1024], P(None, ('fsdp', 'tp')), may hold values from -6 to 6
- segment_ids: int32 [2, 4, 256], P(None, 'fsdp'), may hold values from 0 to 3, never falling along the last dimension, each value on 1 to 128 neighbouring positions
- routes: int32 [2, 2, 1024, 8], P('section', None, 'fsdp'), may hold values from 0 to 31, all different within a row; in each aligned block of 256 rows (0 to 255, 256 to 511, ..., all dimensions but the last counted through in order) at most 128 rows name the same one
- w_query: bfloat16 [2, 1024, 1024], P('section', 'fsdp', 'tp'), may hold values from -0.1875 to 0.1875
- key_weight: bfloat16 [2, 1024, 512], P('section', 'fsdp', 'tp'), may hold values from -0.1875 to 0.1875
- value_weight: bfloat16 [2, 1024, 512], P('section', 'fsdp', 'tp'), may hold values from -0.1875 to 0.1875
- w_output: bfloat16 [2, 1024, 1024], P('section', ('tp', 'fsdp')), may hold values from -1.5 to 1.5
- w_router: bfloat16 [2, 1024, 32], P('section', 'fsdp'), may hold values from -0.375 to 0.375
- gain_attn: float32 [2, 1024], P('section', 'fsdp'), may hold values from 0.5 to 1.5
- gain_moe: float32 [2, 1024], P('section', 'fsdp'), may hold values from 0.5 to 1.5
- w_gate: bfloat16 [2, 32, 1024, 512], P('section', None, 'fsdp', 'tp'), may hold values from -0.1875 to 0.1875
- w_up: bfloat16 [2, 32, 1024, 512], P('section', None, 'fsdp', 'tp'), may hold values from -0.1875 to 0.1875
- w_down: bfloat16 [2, 32, 512, 1024], P('section', None, ('tp', 'fsdp')), may hold values from -1 to 1
- out_grad: bfloat16 [2, 1024, 1024], P(None, ('fsdp', 'tp')), may hold values from -6 to 6
Outputs:
- layer_outputs: bfloat16 [2, 2, 1024, 1024], P('section', None, ('fsdp', 'tp'))
- input_grads: float32 [2, 2, 1024, 1024], P('section', None, ('fsdp', 'tp'))
- w_query_grad: float32 [2, 1024, 1024], P('section', 'fsdp', 'tp')
- w_key_grad: float32 [2, 1024, 512], P('section', 'fsdp', 'tp')
- w_value_grad: float32 [2, 1024, 512], P('section', 'fsdp', 'tp')
- w_output_grad: float32 [2, 1024, 1024], P('section', ('tp', 'fsdp'))
- w_router_grad: float32 [2, 1024, 32], P('section', 'fsdp')
- gain_attn_grad: float32 [2, 1024], P('section', 'fsdp')
- gain_moe_grad: float32 [2, 1024], P('section', 'fsdp')
- w_gate_grad: float32 [2, 32, 1024, 512], P('section', None, 'fsdp', 'tp')
- w_up_grad: float32 [2, 32, 1024, 512], P('section', None, 'fsdp', 'tp')
- w_down_grad: float32 [2, 32, 512, 1024], P('section', None, ('tp', 'fsdp'))
Inputs may be any that keep to these rules, and one draw needn't show every extreme that they name: `segment_ids`: within a group the numbers never fall; each sequence has 1 to 128 tokens and one has exactly 128. `routes`: A token names 8 different experts; the 256 tokens of one group name no expert more than 128 times in one layer, a bound that some block reaches.
All inputs are finite; a program needn't handle non-finite values.
Results may differ from a plain program's by a relative error of at most 0.04.
Values may be sent and summed in bfloat16 or wider, within the bound.
A program may use at most 384 MiB of HBM per device.

v0:
```python
import jax
import jax.numpy as jnp
from jax import lax
from jax.sharding import PartitionSpec as P

QUERY_HEADS = 16
KEY_VALUE_HEADS = 8
HEAD_SIZE = 64
E = 32
TOP = 8
CAP = 128


norm_eps = 1e-06
branch_scale = 0.22
score_scale = 0.015625
rope_base = 10000.0
masked_score = -1e30


def from_behind(array, axis, by):
    count = lax.axis_size(axis)
    pairs = [(i, i + by) for i in range(count) if 0 <= i + by < count]
    return lax.ppermute(array, axis, pairs)


def shortened(array):
    return jax.tree.map(lambda a: a.astype(jnp.bfloat16) if a.dtype == jnp.float32 else a, array)


def norm_rows(vectors, gain_vec):
    inverse = lax.rsqrt(jnp.mean(vectors * vectors, axis=-1, keepdims=True) + norm_eps)
    normed = vectors * inverse
    return (normed * gain_vec, normed, inverse)


def norm_back(upstream, normed, inverse, gain_vec):
    scaled_grad = upstream * gain_vec
    gain_grad = jnp.sum(upstream * normed, axis=0)
    inner_mean = jnp.mean(scaled_grad * normed, axis=-1, keepdims=True)
    return (inverse * (scaled_grad - normed * inner_mean), gain_grad)


def rope_tables(segment):
    position = jnp.arange(segment.shape[0], dtype=jnp.int32)
    before = jnp.concatenate([jnp.full((1,), -1, dtype=jnp.int32), segment[:-1]])
    starts = jnp.where(segment != before, position, jnp.zeros_like(position))
    offsets = (position - lax.cummax(starts, axis=0)).astype(jnp.float32)
    half_dim = HEAD_SIZE // 2
    frequency = rope_base ** (-(jnp.arange(half_dim, dtype=jnp.float32) * 2.0 / HEAD_SIZE))
    angles = offsets[:, None] * frequency[None, :]
    return (jnp.cos(angles)[:, None, :], jnp.sin(angles)[:, None, :])


def rotate(vectors, cosine, sine):
    half_dim = vectors.shape[-1] // 2
    front_half = vectors[..., :half_dim]
    back_half = vectors[..., half_dim:]
    return jnp.concatenate(
        [front_half * cosine - back_half * sine, back_half * cosine + front_half * sine], axis=-1
    )


def rotate_back(vectors, cosine, sine):
    half_dim = vectors.shape[-1] // 2
    front_half = vectors[..., :half_dim]
    back_half = vectors[..., half_dim:]
    return jnp.concatenate(
        [front_half * cosine + back_half * sine, back_half * cosine - front_half * sine], axis=-1
    )


def allowed_pairs(segment):
    position = jnp.arange(segment.shape[0], dtype=jnp.int32)
    return (segment[:, None] == segment[None, :]) & (position[None, :] <= position[:, None])


def route_tables(route):
    flat_routes = route.reshape(-1)
    onehot = (flat_routes[:, None] == jnp.arange(E, dtype=jnp.int32)[None, :]).astype(jnp.int32)
    rank_list = jnp.sum((jnp.cumsum(onehot, axis=0) - 1) * onehot, axis=1)
    slot_index = flat_routes * CAP + rank_list
    owners = jnp.arange(flat_routes.shape[0], dtype=jnp.int32) // TOP
    source = jnp.zeros((E * CAP,), jnp.int32).at[slot_index].set(owners)
    filled = jnp.zeros((E * CAP,), jnp.int32).at[slot_index].set(jnp.ones_like(owners))
    return (slot_index, source, filled)


def dispatch(rows_in, source, filled):
    picked = jnp.take(rows_in, source, axis=0)
    picked = jnp.where(filled[:, None] == 1, picked, jnp.zeros_like(picked))
    return picked.reshape(E, CAP, rows_in.shape[1])


def collect(slot_rows, slot_index):
    flat_rows = slot_rows.reshape(E * CAP, slot_rows.shape[-1])
    return jnp.take(flat_rows, slot_index, axis=0).reshape(-1, TOP, slot_rows.shape[-1]).sum(axis=1)


def place_shares(route_share, slot_index):
    return (
        jnp.zeros((E * CAP,), jnp.float32)
        .at[slot_index]
        .set(route_share.reshape(-1))
        .reshape(E, CAP)
    )


def attend(query_rows, key_matrix, value_matrix, permitted_mask):
    scores = (
        jnp.einsum("qhgd,khd->hgqk", query_rows, key_matrix, preferred_element_type=jnp.float32)
        * score_scale
    )
    scores = jnp.where(permitted_mask[None, None], scores, masked_score)
    row_max = jnp.max(scores, axis=-1, keepdims=True)
    log_sum_exp = row_max + jnp.log(jnp.sum(jnp.exp(scores - row_max), axis=-1, keepdims=True))
    weights_low = jnp.exp(scores - log_sum_exp).astype(jnp.bfloat16)
    attended = jnp.einsum(
        "hgqk,khd->qhgd", weights_low, value_matrix, preferred_element_type=jnp.float32
    )
    return (attended.astype(jnp.bfloat16), log_sum_exp)


def attention_backward(
    query_rows, key_matrix, value_matrix, permitted_mask, log_sum_exp, head_gradient
):
    scores = (
        jnp.einsum("qhgd,khd->hgqk", query_rows, key_matrix, preferred_element_type=jnp.float32)
        * score_scale
    )
    scores = jnp.where(permitted_mask[None, None], scores, masked_score)
    weights_full = jnp.exp(scores - log_sum_exp)
    weights_low = weights_full.astype(jnp.bfloat16)
    value_gradient = jnp.einsum(
        "hgqk,qhgd->khd", weights_low, head_gradient, preferred_element_type=jnp.float32
    )
    weight_grad = jnp.einsum(
        "qhgd,khd->hgqk", head_gradient, value_matrix, preferred_element_type=jnp.float32
    )
    inner_sum = jnp.sum(weights_full * weight_grad, axis=-1, keepdims=True)
    score_grad = (weights_full * (weight_grad - inner_sum) * score_scale).astype(jnp.bfloat16)
    query_gradient = jnp.einsum(
        "hgqk,khd->qhgd", score_grad, key_matrix, preferred_element_type=jnp.float32
    )
    key_gradient = jnp.einsum(
        "hgqk,qhgd->khd", score_grad, query_rows, preferred_element_type=jnp.float32
    )
    return (query_gradient, key_gradient, value_gradient)


def experts_forward(routed, slot_share, gate_up, w_down):
    hidden_units = w_down.shape[1]
    both_pre = jnp.einsum("ecd,edf->ecf", routed, gate_up, preferred_element_type=jnp.float32)
    gate_pre = both_pre[..., :hidden_units]
    up_pre = both_pre[..., hidden_units:]
    hidden = gate_pre * jax.nn.sigmoid(gate_pre) * up_pre
    weighted = (slot_share[:, :, None] * hidden).astype(jnp.bfloat16)
    slot_out = jnp.einsum("ecf,efd->ecd", weighted, w_down, preferred_element_type=jnp.float32)
    return (slot_out, gate_pre, up_pre)


def experts_backward(slot_share, gate_pre, up_pre, slot_grad, gate_up, w_down):
    hidden_grad = jnp.einsum("ecd,efd->ecf", slot_grad, w_down, preferred_element_type=jnp.float32)
    sigmoid_gate = jax.nn.sigmoid(gate_pre)
    hidden = gate_pre * sigmoid_gate * up_pre
    share_slot = jnp.sum(hidden_grad * hidden, axis=-1)
    scaled_grad = slot_share[:, :, None] * hidden_grad
    gate_grad = (
        scaled_grad * up_pre * sigmoid_gate * (1.0 + gate_pre * (1.0 - sigmoid_gate))
    ).astype(jnp.bfloat16)
    up_grad = (scaled_grad * gate_pre * sigmoid_gate).astype(jnp.bfloat16)
    both_grad = jnp.concatenate([gate_grad, up_grad], axis=-1)
    routed_grad = jnp.einsum("ecf,edf->ecd", both_grad, gate_up, preferred_element_type=jnp.float32)
    weighted = (slot_share[:, :, None] * hidden).astype(jnp.bfloat16)
    return (routed_grad, share_slot, both_grad, weighted)


def forward_layer(layer_in, segment, route, weights, gate_up, active):
    (
        w_query,
        key_weight,
        value_weight,
        w_output,
        w_router,
        gain_attn,
        gain_moe,
        w_gate,
        w_up,
        w_down,
    ) = weights
    key_value_heads = key_weight.shape[1] // HEAD_SIZE
    hidden_units = w_gate.shape[2]
    residual = layer_in.astype(jnp.float32)
    scaled_one, normed_one, inverse_one = norm_rows(residual, gain_attn)
    attn_in = lax.all_gather(scaled_one.astype(jnp.bfloat16), "tp", axis=0, tiled=True)
    count_of_tokens = attn_in.shape[0]
    cosine, sine = rope_tables(segment)
    permitted_mask = allowed_pairs(segment)
    query_rows = rotate(
        jnp.dot(attn_in, w_query, preferred_element_type=jnp.float32).reshape(
            count_of_tokens, -1, HEAD_SIZE
        ),
        cosine,
        sine,
    )
    query_rows = query_rows.astype(jnp.bfloat16).reshape(
        count_of_tokens, key_value_heads, QUERY_HEADS // KEY_VALUE_HEADS, HEAD_SIZE
    )
    key_matrix = rotate(
        jnp.dot(attn_in, key_weight, preferred_element_type=jnp.float32).reshape(
            count_of_tokens, key_value_heads, HEAD_SIZE
        ),
        cosine,
        sine,
    ).astype(jnp.bfloat16)
    value_matrix = (
        jnp.dot(attn_in, value_weight, preferred_element_type=jnp.float32)
        .astype(jnp.bfloat16)
        .reshape(count_of_tokens, key_value_heads, HEAD_SIZE)
    )
    attended, log_sum_exp = attend(query_rows, key_matrix, value_matrix, permitted_mask)
    mixed_heads = attended.reshape(count_of_tokens, -1)
    attn_out = lax.psum_scatter(
        jnp.dot(mixed_heads, w_output, preferred_element_type=jnp.float32).astype(jnp.bfloat16),
        "tp",
        scatter_dimension=0,
        tiled=True,
    ).astype(jnp.float32)
    hidden_state = residual + branch_scale * attn_out
    scaled_two, normed_two, inverse_two = norm_rows(hidden_state, gain_moe)
    moe_in = lax.all_gather(scaled_two.astype(jnp.bfloat16), "tp", axis=0, tiled=True)
    logits = jnp.dot(moe_in, w_router, preferred_element_type=jnp.float32)
    route_share = jax.nn.softmax(jnp.take_along_axis(logits, route, axis=1), axis=-1)
    slot_index, source, filled = route_tables(route)
    slot_share = place_shares(route_share, slot_index)

    def expert_pass(operands):
        rows_in, slot_shares = operands
        routed = dispatch(rows_in, source, filled)
        slot_out, gate_pre, up_pre = experts_forward(routed, slot_shares, gate_up, w_down)
        return (collect(slot_out, slot_index), gate_pre, up_pre, routed)

    def expert_skip(operands):
        rows_in = operands[0]
        empty_slots = jnp.zeros((E, CAP, hidden_units), jnp.float32)
        return (
            jnp.zeros(rows_in.shape, jnp.float32),
            empty_slots,
            empty_slots,
            jnp.zeros((E, CAP, rows_in.shape[1]), jnp.bfloat16),
        )

    combined, gate_pre, up_pre, routed = lax.cond(
        active, expert_pass, expert_skip, (moe_in, slot_share)
    )
    moe_out = lax.psum_scatter(
        combined.astype(jnp.bfloat16), "tp", scatter_dimension=0, tiled=True
    ).astype(jnp.float32)
    result = (hidden_state + branch_scale * moe_out).astype(jnp.bfloat16)
    kept_state = (
        attn_in,
        query_rows,
        key_matrix,
        value_matrix,
        attended,
        log_sum_exp,
        normed_one,
        inverse_one,
        normed_two,
        inverse_two,
        moe_in,
        route_share,
        slot_share,
        slot_index,
        source,
        filled,
        gate_pre,
        up_pre,
        cosine,
        sine,
        permitted_mask,
        route,
        routed,
    )
    return (result, kept_state)


def backward_layer(upstream, kept_state, weights, gate_up, active, tp_index):
    (
        w_query,
        key_weight,
        value_weight,
        w_output,
        w_router,
        gain_attn,
        gain_moe,
        w_gate,
        w_up,
        w_down,
    ) = weights
    (
        attn_in,
        query_rows,
        key_matrix,
        value_matrix,
        attended,
        log_sum_exp,
        normed_one,
        inverse_one,
        normed_two,
        inverse_two,
        moe_in,
        route_share,
        slot_share,
        slot_index,
        source,
        filled,
        gate_pre,
        up_pre,
        cosine,
        sine,
        permitted_mask,
        route,
        routed,
    ) = kept_state
    local_rows = upstream.shape[0]
    count_of_tokens = moe_in.shape[0]
    key_value_heads = key_matrix.shape[1]
    hidden_units = w_gate.shape[2]
    moe_grad = lax.all_gather(
        (branch_scale * upstream).astype(jnp.bfloat16), "tp", axis=0, tiled=True
    )

    def expert_back(operands):
        grad_rows, slot_shares, gate_in, up_in = operands
        slot_grad = dispatch(grad_rows, source, filled)
        routed_grad, share_slot, both_grad, weighted = experts_backward(
            slot_shares, gate_in, up_in, slot_grad, gate_up, w_down
        )
        return (collect(routed_grad, slot_index), share_slot, both_grad, weighted, slot_grad)

    def expert_none(operands):
        grad_rows = operands[0]
        narrow = jnp.zeros((E, CAP, hidden_units), jnp.bfloat16)
        paired_zeros = jnp.zeros((E, CAP, 2 * hidden_units), jnp.bfloat16)
        wide = jnp.zeros((E, CAP, grad_rows.shape[1]), jnp.bfloat16)
        return (
            jnp.zeros(grad_rows.shape, jnp.float32),
            jnp.zeros((E, CAP), jnp.float32),
            paired_zeros,
            narrow,
            wide,
        )

    token_grad, share_slot, both_grad, weighted, slot_grad = lax.cond(
        active, expert_back, expert_none, (moe_grad, slot_share, gate_pre, up_pre)
    )
    share_part = jnp.take(share_slot.reshape(-1), slot_index).reshape(count_of_tokens, TOP)
    share_grad = lax.psum(share_part, "tp")
    chosen_grad = route_share * (
        share_grad - jnp.sum(route_share * share_grad, axis=-1, keepdims=True)
    )
    onehot = (route[:, :, None] == jnp.arange(E, dtype=jnp.int32)[None, None, :]).astype(
        jnp.float32
    )
    logit_grad = jnp.einsum("tr,tre->te", chosen_grad, onehot).astype(jnp.bfloat16)
    router_w = jnp.einsum("td,te->de", moe_in, logit_grad, preferred_element_type=jnp.float32)
    own_logits = lax.dynamic_slice_in_dim(logit_grad, tp_index * local_rows, local_rows, 0)
    norm_grad = lax.psum_scatter(
        token_grad.astype(jnp.bfloat16), "tp", scatter_dimension=0, tiled=True
    ).astype(jnp.float32)
    norm_grad = norm_grad + jnp.dot(own_logits, w_router.T, preferred_element_type=jnp.float32)
    back_two, gain_two = norm_back(norm_grad, normed_two, inverse_two, gain_moe)
    hidden_grad = upstream + back_two
    attn_grad = lax.all_gather(
        (branch_scale * hidden_grad).astype(jnp.bfloat16), "tp", axis=0, tiled=True
    )
    mixed_heads = attended.reshape(count_of_tokens, -1)
    head_gradient = jnp.dot(attn_grad, w_output.T, preferred_element_type=jnp.float32).astype(
        jnp.bfloat16
    )
    output_w = jnp.einsum("tk,td->kd", mixed_heads, attn_grad, preferred_element_type=jnp.float32)
    query_gradient, key_gradient, value_gradient = attention_backward(
        query_rows,
        key_matrix,
        value_matrix,
        permitted_mask,
        log_sum_exp,
        head_gradient.reshape(
            count_of_tokens, key_value_heads, QUERY_HEADS // KEY_VALUE_HEADS, HEAD_SIZE
        ),
    )
    query_gradient = (
        rotate_back(query_gradient.reshape(count_of_tokens, -1, HEAD_SIZE), cosine, sine)
        .reshape(count_of_tokens, -1)
        .astype(jnp.bfloat16)
    )
    key_gradient = (
        rotate_back(key_gradient, cosine, sine).reshape(count_of_tokens, -1).astype(jnp.bfloat16)
    )
    value_gradient = value_gradient.reshape(count_of_tokens, -1).astype(jnp.bfloat16)
    query_w = jnp.einsum("td,tk->dk", attn_in, query_gradient, preferred_element_type=jnp.float32)
    key_w = jnp.einsum("td,tk->dk", attn_in, key_gradient, preferred_element_type=jnp.float32)
    value_w = jnp.einsum("td,tk->dk", attn_in, value_gradient, preferred_element_type=jnp.float32)
    input_part = jnp.dot(query_gradient, w_query.T, preferred_element_type=jnp.float32)
    input_part = input_part + jnp.dot(
        key_gradient, key_weight.T, preferred_element_type=jnp.float32
    )
    input_part = input_part + jnp.dot(
        value_gradient, value_weight.T, preferred_element_type=jnp.float32
    )
    norm_one_grad = lax.psum_scatter(
        input_part.astype(jnp.bfloat16), "tp", scatter_dimension=0, tiled=True
    ).astype(jnp.float32)
    back_one, gain_one = norm_back(norm_one_grad, normed_one, inverse_one, gain_attn)
    tick_grads = (query_w, key_w, value_w, output_w, router_w, gain_one, gain_two)
    return (hidden_grad + back_one, tick_grads, (routed, both_grad, weighted, slot_grad))


def reduce_grads(attn_parts, expert_parts):
    query_w, key_w, value_w, output_w, router_w, gain_one, gain_two = attn_parts
    gate_w, up_w, down_w = expert_parts
    gain_one, gain_two = lax.psum((gain_one, gain_two), "tp")
    return (
        lax.psum_scatter(
            query_w.astype(jnp.bfloat16), "fsdp", scatter_dimension=0, tiled=True
        ).astype(jnp.float32),
        lax.psum_scatter(
            key_w.astype(jnp.bfloat16), "fsdp", scatter_dimension=0, tiled=True
        ).astype(jnp.float32),
        lax.psum_scatter(
            value_w.astype(jnp.bfloat16), "fsdp", scatter_dimension=0, tiled=True
        ).astype(jnp.float32),
        lax.psum_scatter(
            output_w.astype(jnp.bfloat16), "fsdp", scatter_dimension=0, tiled=True
        ).astype(jnp.float32),
        lax.psum_scatter(
            router_w.astype(jnp.bfloat16), "fsdp", scatter_dimension=0, tiled=True
        ).astype(jnp.float32),
        lax.psum_scatter(
            gain_one.astype(jnp.bfloat16), "fsdp", scatter_dimension=0, tiled=True
        ).astype(jnp.float32),
        lax.psum_scatter(
            gain_two.astype(jnp.bfloat16), "fsdp", scatter_dimension=0, tiled=True
        ).astype(jnp.float32),
        lax.psum_scatter(
            gate_w.astype(jnp.bfloat16), "fsdp", scatter_dimension=1, tiled=True
        ).astype(jnp.float32),
        lax.psum_scatter(up_w.astype(jnp.bfloat16), "fsdp", scatter_dimension=1, tiled=True).astype(
            jnp.float32
        ),
        lax.psum_scatter(
            down_w.astype(jnp.bfloat16), "fsdp", scatter_dimension=1, tiled=True
        ).astype(jnp.float32),
    )


def per_device(
    inputs,
    segment_ids,
    routes,
    w_query,
    key_weight,
    value_weight,
    w_output,
    w_router,
    gain_attn,
    gain_moe,
    w_gate,
    w_up,
    w_down,
    out_grad,
):
    section_count = lax.axis_size("section")
    section_index = lax.axis_index("section")
    tp_index = lax.axis_index("tp")
    micro_count = inputs.shape[0]
    local_rows = inputs.shape[1]
    model_width = inputs.shape[2]
    weights = (
        lax.all_gather(w_query[0], "fsdp", axis=0, tiled=True),
        lax.all_gather(key_weight[0], "fsdp", axis=0, tiled=True),
        lax.all_gather(value_weight[0], "fsdp", axis=0, tiled=True),
        lax.all_gather(w_output[0], "fsdp", axis=0, tiled=True),
        lax.all_gather(w_router[0], "fsdp", axis=0, tiled=True),
        lax.all_gather(gain_attn[0].astype(jnp.bfloat16), "fsdp", axis=0, tiled=True).astype(
            jnp.float32
        ),
        lax.all_gather(gain_moe[0].astype(jnp.bfloat16), "fsdp", axis=0, tiled=True).astype(
            jnp.float32
        ),
        lax.all_gather(w_gate[0], "fsdp", axis=1, tiled=True),
        lax.all_gather(w_up[0], "fsdp", axis=1, tiled=True),
        lax.all_gather(w_down[0], "fsdp", axis=1, tiled=True),
    )
    gate_up = jnp.concatenate([weights[7], weights[8]], axis=2)
    segment_rows = segment_ids[:, 0, :]
    route_rows = routes[0]
    tick_count = micro_count + section_count - 1
    outputs = jnp.zeros((micro_count, local_rows, model_width), jnp.bfloat16)
    history = []
    previous = None
    for tick_step in range(tick_count):
        mb_index = tick_step - section_index
        active = (mb_index >= 0) & (mb_index < micro_count)
        mb_pick = jnp.clip(mb_index, 0, micro_count - 1)
        fresh_input = inputs[min(tick_step, micro_count - 1)]
        if previous is None:
            arrived = jnp.zeros_like(fresh_input)
        else:
            arrived = from_behind(previous, "section", 1)
        layer_in = jnp.where(section_index == 0, fresh_input, arrived)
        segment = lax.dynamic_index_in_dim(segment_rows, mb_pick, 0, keepdims=False)
        route = lax.dynamic_index_in_dim(route_rows, mb_pick, 0, keepdims=False)
        result, kept_state = forward_layer(layer_in, segment, route, weights, gate_up, active)
        outputs = jnp.where(
            active, lax.dynamic_update_index_in_dim(outputs, result, mb_pick, 0), outputs
        )
        history.append(kept_state)
        previous = result
    model_full = weights[7].shape[1]
    hidden_units = weights[7].shape[2]
    attn_sums = tuple((jnp.zeros(matrix.shape, jnp.float32) for matrix in weights[:7]))
    wide_store = jnp.zeros((micro_count + 1, E, CAP, model_full), jnp.bfloat16)
    paired_store = jnp.zeros((micro_count + 1, E, CAP, 2 * hidden_units), jnp.bfloat16)
    narrow_store = jnp.zeros((micro_count + 1, E, CAP, hidden_units), jnp.bfloat16)
    term_stores = (wide_store, paired_store, narrow_store, wide_store)
    input_grads = jnp.zeros((micro_count, local_rows, model_width), jnp.float32)
    previous = None
    for tick_step in range(tick_count):
        mb_index = micro_count + section_count - 2 - tick_step - section_index
        active = (mb_index >= 0) & (mb_index < micro_count)
        mb_pick = jnp.clip(mb_index, 0, micro_count - 1)
        fresh_grad = out_grad[max(micro_count - 1 - tick_step, 0)].astype(jnp.float32)
        if previous is None:
            arrived = jnp.zeros_like(fresh_grad)
        else:
            arrived = from_behind(shortened(previous), "section", -1).astype(previous.dtype)
        upstream = jnp.where(section_index == section_count - 1, fresh_grad, arrived)
        grad_out, tick_grads, terms = backward_layer(
            upstream, history[tick_count - 1 - tick_step], weights, gate_up, active, tp_index
        )
        input_grads = jnp.where(
            active, lax.dynamic_update_index_in_dim(input_grads, grad_out, mb_pick, 0), input_grads
        )
        tick_grads = tuple((jnp.where(active, part, jnp.zeros_like(part)) for part in tick_grads))
        attn_sums = tuple((total + part for total, part in zip(attn_sums, tick_grads)))
        slot_pick = jnp.where(active, mb_pick, micro_count)
        term_stores = tuple(
            (
                lax.dynamic_update_index_in_dim(store, term, slot_pick, 0)
                for store, term in zip(term_stores, terms)
            )
        )
        previous = grad_out
    routed, both_grad, weighted, slot_grad = term_stores
    both_w = jnp.einsum("mecd,mecf->edf", routed, both_grad, preferred_element_type=jnp.float32)
    down_w = jnp.einsum("mecf,mecd->efd", weighted, slot_grad, preferred_element_type=jnp.float32)
    shard_sums = reduce_grads(
        attn_sums, (both_w[..., :hidden_units], both_w[..., hidden_units:], down_w)
    )
    return (outputs[None], input_grads[None]) + tuple((part[None] for part in shard_sums))


def solution(mesh):
    in_specs = (
        P(None, ("fsdp", "tp"), None),
        P(None, "fsdp", None),
        P("section", None, "fsdp", None),
        P("section", "fsdp", "tp"),
        P("section", "fsdp", "tp"),
        P("section", "fsdp", "tp"),
        P("section", ("tp", "fsdp"), None),
        P("section", "fsdp", None),
        P("section", "fsdp"),
        P("section", "fsdp"),
        P("section", None, "fsdp", "tp"),
        P("section", None, "fsdp", "tp"),
        P("section", None, ("tp", "fsdp"), None),
        P(None, ("fsdp", "tp"), None),
    )
    out_specs = (
        P("section", None, ("fsdp", "tp"), None),
        P("section", None, ("fsdp", "tp"), None),
        P("section", "fsdp", "tp"),
        P("section", "fsdp", "tp"),
        P("section", "fsdp", "tp"),
        P("section", ("tp", "fsdp"), None),
        P("section", "fsdp", None),
        P("section", "fsdp"),
        P("section", "fsdp"),
        P("section", None, "fsdp", "tp"),
        P("section", None, "fsdp", "tp"),
        P("section", None, ("tp", "fsdp"), None),
    )
    return jax.shard_map(
        per_device, mesh=mesh, in_specs=in_specs, out_specs=out_specs, check_vma=False
    )
```

profile of v0, /device:TPU:0, one launch (start us, length us, event | category | flops | bytes accessed | tf_op | source)
XLA Modules:
  0.0 2073.9 jit_solution(15176877856943159653)
XLA Ops:
  10.3 12.6 all-gather
  32.2 14.8 all-gather.1
  47.0 14.9 all-gather.3
  64.6 14.3 all-gather.2
  81.2 14.8 all-gather.4
  110.6 10.0 all-gather.5
  137.3 17.0 all-gather.6
  164.0 16.8 gather_fusion.12
  189.4 59.5 %all-gather.16.cloned.1.call-done = bf16[1,32,1024,128]{3,2,1,0:T(8,128)(2,1)} async-done(((bf16[1,32,256,128]{3,2,1,0:T(8,128)(2,1)}), bf16[1,32,1024,128]{3,2,1,0:T(8,128)(2,1)}) %all-gather.16.cloned.1.call-update) | async-done | bytes 8388624 | tf_op jit(solution)/shard_map/all_gather | solution.py:493
  248.9 149.2 %all-gather.14.cloned.1.call-done = bf16[1,32,1024,128]{3,2,1,0:T(8,128)(2,1)} async-done(((bf16[1,32,256,128]{3,2,1,0:T(8,128)(2,1)}), bf16[1,32,1024,128]{3,2,1,0:T(8,128)(2,1)}) %all-gather.14.cloned.1.call-update) | async-done | bytes 8388624 | tf_op jit(solution)/shard_map/all_gather | solution.py:492
  398.1 14.3 pad_maximum_fusion.6
  412.4 134.9 %all-gather.18.cloned.1.call-done = bf16[1,32,128,1024]{3,2,1,0:T(8,128)(2,1)} async-done(((bf16[1,32,32,1024]{3,2,1,0:T(8,128)(2,1)}), bf16[1,32,128,1024]{3,2,1,0:T(8,128)(2,1)}) %all-gather.18.cloned.1.call-update) | async-done | bytes 8388624 | tf_op jit(solution)/shard_map/all_gather | solution.py:494
  547.3 76.5 %conditional.6 = (bf16[256,1024]{1,0:T(8,128)(2,1)S(1)}, f32[32,128,128]{2,1,0:T(8,128)}, f32[32,128,128]{2,1,0:T(8,128)}, bf16[1,32,128,1024]{3,2,1,0:T(8,128)(2,1)}) conditional(s32[]{:T(128)} %convert_element_type.432, () %tuple.90, (f32[4096]{0:T(1024)S(1)}, s32[4096]{0:T(1024)S(1)}, bf16[256,1024]{1,0:T(8,128)(2,1)S(1)}, s32[4096]{0:T(1024)S(1)}, ...), branch_computations={%region_15.17_spmd, %region_16.21_spmd} | conditional | flops 3237281792 | bytes 151670864 | solution.py:253
  547.7 18.2 gather_fusion
  573.8 12.7 fusion.308
  591.2 10.4 fusion
  601.6 17.4 gather_fusion.1
  703.1 16.8 gather_fusion.13
  729.3 77.0 %conditional.7 = (bf16[256,1024]{1,0:T(8,128)(2,1)S(1)}, f32[32,128,128]{2,1,0:T(8,128)}, f32[32,128,128]{2,1,0:T(8,128)}, bf16[1,32,128,1024]{3,2,1,0:T(8,128)(2,1)}) conditional(s32[]{:T(128)} %convert_element_type.450, () %tuple.92, (f32[4096]{0:T(1024)}, s32[4096]{0:T(1024)}, bf16[256,1024]{1,0:T(8,128)(2,1)S(1)}, s32[4096]{0:T(1024)}, ...), branch_computations={%region_34.38_spmd, %region_35.40_spmd} | conditional | flops 3237281792 | bytes 151900352 | solution.py:253
  730.1 18.2 gather_fusion.2
  756.1 12.7 fusion.309
  773.6 10.4 fusion.6
  784.0 17.4 gather_fusion.3
  807.2 23.4 %reduce-scatter.27.cloned.1.call-done = bf16[64,1024]{1,0:T(8,128)(2,1)} async-done(((bf16[256,1024]{1,0:T(8,128)(2,1)}), bf16[64,1024]{1,0:T(8,128)(2,1)}) %reduce-scatter.27.cloned.1.call-update) | async-done | bytes 131088 | tf_op jit(solution)/shard_map/reduce_scatter | solution.py:256
  884.9 16.8 gather_fusion.14
  926.0 11.8 gather_fusion.15
  944.9 146.1 %reduce-scatter.33.cloned.1.call-done = bf16[64,1024]{1,0:T(8,128)(2,1)} async-done(((bf16[256,1024]{1,0:T(8,128)(2,1)}), bf16[64,1024]{1,0:T(8,128)(2,1)}) %reduce-scatter.33.cloned.1.call-update) | async-done | bytes 131088 | tf_op jit(solution)/shard_map/reduce_scatter | solution.py:369
  1113.9 22.4 %reduce-scatter.35.cloned.1.call-done = bf16[64,1024]{1,0:T(8,128)(2,1)} async-done(((bf16[256,1024]{1,0:T(8,128)(2,1)}), bf16[64,1024]{1,0:T(8,128)(2,1)}) %reduce-scatter.35.cloned.1.call-update) | async-done | bytes 131088 | tf_op jit(solution)/shard_map/reduce_scatter | solution.py:412
  1152.5 85.7 %conditional.10 = (bf16[256,1024]{1,0:T(8,128)(2,1)}, f32[4096]{0:T(1024)S(1)}, bf16[1,32,128,128]{2,3,1,0:T(8,128)(2,1)}, bf16[1,32,128,1024]{3,2,1,0:T(8,128)(2,1)}, bf16[1,32,128,256]{3,2,0,1:T(8,128)(2,1)}) conditional(s32[]{:T(128)} %convert_element_type.450, () %tuple.98, (f32[4096]{0:T(1024)}, s32[4096]{0:T(1024)}, ...), branch_computations={%region_68.73_spmd, %region_69.76_spmd} | conditional | flops 3252482048 | bytes 140382368 | solution.py:355
  1158.5 18.2 gather_fusion.8
  1184.2 12.4 multiply_reduce_fusion.1
  1196.6 12.8 fusion.25
  1209.4 17.4 gather_fusion.9
  1239.2 11.8 gather_fusion.16
  1283.6 21.5 %reduce-scatter.39.cloned.1.call-done = bf16[64,1024]{1,0:T(8,128)(2,1)} async-done(((bf16[256,1024]{1,0:T(8,128)(2,1)}), bf16[64,1024]{1,0:T(8,128)(2,1)}) %reduce-scatter.39.cloned.1.call-update) | async-done | bytes 131088 | tf_op jit(solution)/shard_map/reduce_scatter | solution.py:412
  1321.4 85.0 %conditional.11 = (bf16[256,1024]{1,0:T(8,128)(2,1)S(1)}, f32[4096]{0:T(1024)S(1)}, bf16[1,32,128,128]{2,3,1,0:T(8,128)(2,1)}, bf16[1,32,128,1024]{3,2,1,0:T(8,128)(2,1)}, bf16[1,32,128,256]{3,2,0,1:T(8,128)(2,1)}) conditional(s32[]{:T(128)} %convert_element_type.432, () %tuple.100, (f32[4096]{0:T(1024)}, s32[4096]{0:T(1024)}, ...), branch_computations={%region_79.84_spmd, %region_80.87_spmd} | conditional | flops 3252482048 | bytes 140382368 | solution.py:355
  1327.3 18.2 gather_fusion.10
  1353.0 12.6 multiply_reduce_fusion.2
  1365.5 12.8 fusion.31
  1378.4 17.4 gather_fusion.11
  1458.1 12.0 gather_fusion.17
  1526.7 19.9 bitcast_convert_fusion
  1548.1 11.7 fusion.304
  1599.1 13.2 bitcast_convert_fusion.1
  1628.2 12.1 all-reduce.3
  1645.9 121.2 %reduce-scatter.55.cloned.1.call-done = bf16[32,256,128]{2,1,0:T(8,128)(2,1)} async-done(((bf16[32,1024,128]{2,1,0:T(8,128)(2,1)}), bf16[32,256,128]{2,1,0:T(8,128)(2,1)}) %reduce-scatter.55.cloned.1.call-update) | async-done | bytes 2097168 | tf_op jit(solution)/shard_map/reduce_scatter | solution.py:446
  1771.2 143.4 %reduce-scatter.57.cloned.1.call-done = bf16[32,256,128]{2,1,0:T(8,128)(2,1)} async-done(((bf16[32,1024,128]{2,1,0:T(8,128)(2,1)}), bf16[32,256,128]{2,1,0:T(8,128)(2,1)}) %reduce-scatter.57.cloned.1.call-update) | async-done | bytes 2097168 | tf_op jit(solution)/shard_map/reduce_scatter | solution.py:449
  1918.7 143.4 %reduce-scatter.59.cloned.1.call-done = bf16[32,32,1024]{2,1,0:T(8,128)(2,1)} async-done(((bf16[32,128,1024]{2,1,0:T(8,128)(2,1)}), bf16[32,32,1024]{2,1,0:T(8,128)(2,1)}) %reduce-scatter.59.cloned.1.call-update) | async-done | bytes 2097168 | tf_op jit(solution)/shard_map/reduce_scatter | solution.py:452
  (833 shorter events, 608.0 us)
Async XLA Ops:
  8.0 146.9 %reduce-scatter.21.cloned.1.call-start = ((), (), s32[]{:S(2)}) async-start(), calls=%async_computation.20 | async-start | bytes 655360 | tf_op jit(solution)/shard_map/reduce_scatter | solution.py:223
  23.0 628.0 %copy-start.95 = (f32[1,1024]{1,0:T(1,128)}, f32[1,1024]{1,0:T(1,128)S(1)}, u32[]{:S(2)}) copy-start(f32[1,1024]{1,0:T(1,128)S(1)} %convert_element_type.530) | copy-start | bytes 12292
  47.0 797.4 %copy-start.21 = (bf16[1,1024,128]{2,1,0:T(8,128)(2,1)}, bf16[1,1024,128]{2,1,0:T(8,128)(2,1)S(1)}, u32[]{:S(2)}) copy-start(bf16[1,1024,128]{2,1,0:T(8,128)(2,1)S(1)} %all-gather.1) | copy-start | bytes 786436
  61.9 782.8 %copy-start.9 = (bf16[1,1024,256]{2,1,0:T(8,128)(2,1)}, bf16[1,1024,256]{2,1,0:T(8,128)(2,1)S(1)}, u32[]{:S(2)}) copy-start(bf16[1,1024,256]{2,1,0:T(8,128)(2,1)S(1)} %all-gather.3) | copy-start | bytes 1572868
  78.9 766.1 %copy-start.19 = (bf16[1,1024,128]{2,1,0:T(8,128)(2,1)}, bf16[1,1024,128]{2,1,0:T(8,128)(2,1)S(1)}, u32[]{:S(2)}) copy-start(bf16[1,1024,128]{2,1,0:T(8,128)(2,1)S(1)} %all-gather.2) | copy-start | bytes 786436
  80.3 578.5 %copy-start.87 = (f32[256,32]{0,1:T(8,128)}, f32[256,32]{0,1:T(8,128)S(1)}, u32[]{:S(2)}) copy-start(f32[256,32]{0,1:T(8,128)S(1)} %get-tuple-element.427) | copy-start | bytes 98308
  80.3 578.5 %copy-start.89 = (f32[256,32]{0,1:T(8,128)}, f32[256,32]{0,1:T(8,128)S(1)}, u32[]{:S(2)}) copy-start(f32[256,32]{0,1:T(8,128)S(1)} %get-tuple-element.428) | copy-start | bytes 98308
  96.0 751.3 %copy-start.11 = (bf16[1,256,1024]{2,1,0:T(8,128)(2,1)}, bf16[1,256,1024]{2,1,0:T(8,128)(2,1)S(1)}, u32[]{:S(2)}) copy-start(bf16[1,256,1024]{2,1,0:T(8,128)(2,1)S(1)} %all-gather.4) | copy-start | bytes 1572868
  97.4 151.5 %all-gather.16.cloned.1.call-start = ((), (), s32[]{:S(2)}) async-start(), calls=%async_computation.41 | async-start | bytes 10485760 | tf_op jit(solution)/shard_map/all_gather | solution.py:493
  98.0 300.1 %all-gather.14.cloned.1.call-start = ((), (), s32[]{:S(2)}) async-start(), calls=%async_computation.40 | async-start | bytes 10485760 | tf_op jit(solution)/shard_map/all_gather | solution.py:492
  98.6 448.6 %all-gather.18.cloned.1.call-start = ((), (), s32[]{:S(2)}) async-start(), calls=%async_computation.42 | async-start | bytes 10485760 | tf_op jit(solution)/shard_map/all_gather | solution.py:494
  99.2 544.5 %reduce-scatter.23.cloned.1.call-start = ((), (), s32[]{:S(2)}) async-start(), calls=%async_computation.21 | async-start | bytes 655360 | tf_op jit(solution)/shard_map/reduce_scatter | solution.py:256
  99.9 534.7 %copy-start.118 = (s32[1,1,256,8]{2,3,1,0:T(8,128)}, s32[1,1,256,8]{2,3,1,0:T(8,128)S(1)}, u32[]{:S(2)}) copy-start(s32[1,1,256,8]{2,3,1,0:T(8,128)S(1)} %get-tuple-element.342) | copy-start | bytes 24580
  99.9 620.2 %copy-start.116 = (s32[1,1,256,8]{2,3,1,0:T(8,128)}, s32[1,1,256,8]{2,3,1,0:T(8,128)S(1)}, u32[]{:S(2)}) copy-start(s32[1,1,256,8]{2,3,1,0:T(8,128)S(1)} %get-tuple-element.414) | copy-start | bytes 24580
  100.6 563.1 %copy-start.144 = (s32[2048]{0:T(1024)}, s32[2048]{0:T(1024)S(1)}, u32[]{:S(2)}) copy-start(s32[2048]{0:T(1024)S(1)} %eq.234) | copy-start | bytes 24580
  120.6 573.9 %copy-start.131 = (f32[1,1024]{1,0:T(1,128)}, f32[1,1024]{1,0:T(1,128)S(1)}, u32[]{:S(2)}) copy-start(f32[1,1024]{1,0:T(1,128)S(1)} %convert_element_type.531) | copy-start | bytes 12292
  129.2 418.1 %copy-start.134 = (s32[4096]{0:T(1024)}, s32[4096]{0:T(1024)S(1)}, u32[]{:S(2)}) copy-start(s32[4096]{0:T(1024)S(1)} %scatter_custom_fusion.1) | copy-start | bytes 49156
  137.3 409.9 %copy-start.111 = (s32[4096]{0:T(1024)}, s32[4096]{0:T(1024)S(1)}, u32[]{:S(2)}) copy-start(s32[4096]{0:T(1024)S(1)} %scatter_custom_fusion.2) | copy-start | bytes 49156
  154.3 730.3 %copy-start.79 = (bf16[1,1024,32]{1,2,0:T(8,128)(2,1)}, bf16[1,1024,32]{1,2,0:T(8,128)(2,1)S(1)}, u32[]{:S(2)}) copy-start(bf16[1,1024,32]{1,2,0:T(8,128)(2,1)S(1)} %all-gather.6) | copy-start | bytes 196612
  154.9 392.4 %copy-start.121 = (s32[2048]{0:T(1024)}, s32[2048]{0:T(1024)S(1)}, u32[]{:S(2)}) copy-start(s32[2048]{0:T(1024)S(1)} %get-tuple-element.332) | copy-start | bytes 24580
  163.8 383.5 %copy-start = (bf16[256,1024]{1,0:T(8,128)(2,1)}, bf16[256,1024]{1,0:T(8,128)(2,1)S(1)}, u32[]{:S(2)}) copy-start(bf16[256,1024]{1,0:T(8,128)(2,1)S(1)} %all_gather.73) | copy-start | bytes 1572868
  181.1 231.3 %copy-start.139 = (f32[256,8]{0,1:T(8,128)}, f32[256,8]{0,1:T(8,128)S(1)}, u32[]{:S(2)}) copy-start(f32[256,8]{0,1:T(8,128)S(1)} %fusion.260) | copy-start | bytes 24580
  189.4 357.9 %copy-start.148 = (f32[4096]{0:T(1024)}, f32[4096]{0:T(1024)S(1)}, u32[]{:S(2)}) copy-start(f32[4096]{0:T(1024)S(1)} %scatter_custom_fusion) | copy-start | bytes 49156
  624.7 68.8 %reduce-scatter.25.cloned.1.call-start = ((), (), s32[]{:S(2)}) async-start(), calls=%async_computation.22 | async-start | bytes 655360 | tf_op jit(solution)/shard_map/reduce_scatter | solution.py:223
  644.8 6.0 collective-permute-start
  650.9 179.6 %copy-start.24 = (bf16[64,1024]{1,0:T(8,128)(2,1)}, bf16[64,1024]{1,0:T(8,128)(2,1)S(1)}, u32[]{:S(2)}) copy-start(bf16[64,1024]{1,0:T(8,128)(2,1)S(1)} %get-tuple-element.350) | copy-start | bytes 393220
  663.7 166.9 %reduce-scatter.27.cloned.1.call-start = ((), (), s32[]{:S(2)}) async-start(), calls=%async_computation.23 | async-start | bytes 655360 | tf_op jit(solution)/shard_map/reduce_scatter | solution.py:256
  807.1 68.1 %reduce-scatter.29.cloned.1.call-start = ((), (), s32[]{:S(2)}) async-start(), calls=%async_computation.24 | async-start | bytes 655360 | tf_op jit(solution)/shard_map/reduce_scatter | solution.py:223
  831.6 6.0 collective-permute-start.1
  848.4 242.7 %reduce-scatter.33.cloned.1.call-start = ((), (), s32[]{:S(2)}) async-start(), calls=%async_computation.26 | async-start | bytes 655360 | tf_op jit(solution)/shard_map/reduce_scatter | solution.py:369
  925.8 210.5 %reduce-scatter.35.cloned.1.call-start = ((), (), s32[]{:S(2)}) async-start(), calls=%async_computation.27 | async-start | bytes 655360 | tf_op jit(solution)/shard_map/reduce_scatter | solution.py:412
  1113.9 149.1 %reduce-scatter.37.cloned.1.call-start = ((), (), s32[]{:S(2)}) async-start(), calls=%async_computation.28 | async-start | bytes 655360 | tf_op jit(solution)/shard_map/reduce_scatter | solution.py:369
  1139.0 7.0 collective-permute-start.2
  1238.3 66.8 %reduce-scatter.39.cloned.1.call-start = ((), (), s32[]{:S(2)}) async-start(), calls=%async_computation.29 | async-start | bytes 655360 | tf_op jit(solution)/shard_map/reduce_scatter | solution.py:412
  1283.6 200.5 %reduce-scatter.41.cloned.1.call-start = ((), (), s32[]{:S(2)}) async-start(), calls=%async_computation.30 | async-start | bytes 655360 | tf_op jit(solution)/shard_map/reduce_scatter | solution.py:369
  1307.9 7.0 collective-permute-start.3
  1407.2 207.0 %reduce-scatter.31.cloned.1.call-start = ((), (), s32[]{:S(2)}) async-start(), calls=%async_computation.25 | async-start | bytes 655360 | tf_op jit(solution)/shard_map/reduce_scatter | solution.py:256
  1410.5 205.3 %reduce-scatter.53.cloned.1.call-start = ((), (), s32[]{:S(2)}) async-start(), calls=%async_computation.36 | async-start | bytes 81920 | tf_op jit(solution)/shard_map/reduce_scatter | solution.py:437
  1484.0 133.2 %reduce-scatter.47.cloned.1.call-start = ((), (), s32[]{:S(2)}) async-start(), calls=%async_computation.33 | async-start | bytes 327680 | tf_op jit(solution)/shard_map/reduce_scatter | solution.py:428
  1511.2 107.5 %reduce-scatter.49.cloned.1.call-start = ((), (), s32[]{:S(2)}) async-start(), calls=%async_computation.34 | async-start | bytes 327680 | tf_op jit(solution)/shard_map/reduce_scatter | solution.py:431
  1516.3 104.0 %reduce-scatter.43.cloned.1.call-start = ((), (), s32[]{:S(2)}) async-start(), calls=%async_computation.31 | async-start | bytes 655360 | tf_op jit(solution)/shard_map/reduce_scatter | solution.py:412
  1520.0 121.6 %reduce-scatter.45.cloned.1.call-start = ((), (), s32[]{:S(2)}) async-start(), calls=%async_computation.32 | async-start | bytes 655360 | tf_op jit(solution)/shard_map/reduce_scatter | solution.py:425
  1526.7 116.5 %reduce-scatter.51.cloned.1.call-start = ((), (), s32[]{:S(2)}) async-start(), calls=%async_computation.35 | async-start | bytes 655360 | tf_op jit(solution)/shard_map/reduce_scatter | solution.py:434
  1548.1 219.0 %reduce-scatter.55.cloned.1.call-start = ((), (), s32[]{:S(2)}) async-start(), calls=%async_computation.37 | async-start | bytes 10485760 | tf_op jit(solution)/shard_map/reduce_scatter | solution.py:446
  1559.8 354.7 %reduce-scatter.57.cloned.1.call-start = ((), (), s32[]{:S(2)}) async-start(), calls=%async_computation.38 | async-start | bytes 10485760 | tf_op jit(solution)/shard_map/reduce_scatter | solution.py:449
  1560.6 501.5 %reduce-scatter.59.cloned.1.call-start = ((), (), s32[]{:S(2)}) async-start(), calls=%async_computation.39 | async-start | bytes 10485760 | tf_op jit(solution)/shard_map/reduce_scatter | solution.py:452
  1615.3 303.4 %copy-start.129 = (bf16[1,2,64,1024]{3,2,1,0:T(8,128)(2,1)}, bf16[1,2,64,1024]{3,2,1,0:T(8,128)(2,1)S(1)}, u32[]{:S(2)}) copy-start(bf16[1,2,64,1024]{3,2,1,0:T(8,128)(2,1)S(1)} %fusion.222) | copy-start | bytes 786436
  1645.9 420.2 %copy-start.109 = (f32[1,2,64,1024]{3,2,1,0:T(8,128)}, f32[1,2,64,1024]{3,2,1,0:T(8,128)S(1)}, u32[]{:S(2)}) copy-start(f32[1,2,64,1024]{3,2,1,0:T(8,128)S(1)} %fusion.161) | copy-start | bytes 1572868
  (181 other events, 6274.9 us)
Sparse Core Ops, SparseCore 0:
  97.6 20.6 reduce-scatter.20
  624.8 18.9 reduce-scatter.22
  663.8 23.4 reduce-scatter.24
  807.2 23.2 reduce-scatter.26
  848.6 24.3 reduce-scatter.28
  925.9 165.1 reduce-scatter.32
  1114.0 22.2 reduce-scatter.34
  1238.4 21.5 reduce-scatter.36
  1283.7 21.3 reduce-scatter.38
  1407.3 21.3 reduce-scatter.40
  1431.8 21.6 reduce-scatter.30
  1484.2 18.6 reduce-scatter.52
  1511.3 19.6 reduce-scatter.46
  1533.2 18.2 reduce-scatter.48
  1554.3 19.8 reduce-scatter.42
  1576.9 21.8 reduce-scatter.44
  1601.5 20.2 reduce-scatter.50
  1624.0 143.0 reduce-scatter.54
  1769.5 145.0 reduce-scatter.56
  1916.8 145.2 reduce-scatter.58
Sparse Core Ops, SparseCore 1:
  99.5 149.4 all-gather.15
  250.4 147.7 all-gather.13
  399.6 147.6 all-gather.17
where the time goes:
time: 2090 us; the launch traced here: 2070 us
  waiting for transfers between devices  991 us (47%)
  local copies, waits for them, and re-layouts  469 us (22%)
  blocking collectives  221 us (11%)
  matrix products  200 us (10%)
  other arithmetic  160 us (8%)
    all_gather x1, waiting for transfers between devices, per_device(): lax.all_gather(w_gate[0], 'fsdp', axis=1, tiled=True)  149 us
    reduce_scatter x3, waiting for transfers between devices, backward_layer(): lax.psum_scatter(token_grad.astype(jnp.bfloat16), 'tp', scatter_dimension...  146 us
    reduce_scatter x1, waiting for transfers between devices, reduce_grads(): lax.psum_scatter(down_w.astype(jnp.bfloat16), 'fsdp', scatter_dimension=1...  143 us
    reduce_scatter x1, waiting for transfers between devices, reduce_grads(): lax.psum_scatter(up_w.astype(jnp.bfloat16), 'fsdp', scatter_dimension=1,...  143 us
    all_gather x1, waiting for transfers between devices, per_device(): lax.all_gather(w_down[0], 'fsdp', axis=1, tiled=True)  135 us
    reduce_scatter x1, waiting for transfers between devices, reduce_grads(): lax.psum_scatter(gate_w.astype(jnp.bfloat16), 'fsdp', scatter_dimension=1...  121 us
    gather x4, local copies, waits for them, and re-layouts, dispatch(): picked = jnp.take(rows_in, source, axis=0)  72.8 us
    gather x4, local copies, waits for them, and re-layouts, collect(): jnp.take(flat_rows, slot_index, axis=0)  69.7 us
  transfers between devices with their start and end apart: 27, of which 15 were waited for; matrix products, arithmetic and copies ran while one was open for 18% of the time, Pallas kernels for 0%

commit v1 on v0

v1 whole, which is shorter than its diff:
```python
import jax
import jax.numpy as jnp
from jax import lax
from jax.sharding import PartitionSpec as P

QUERY_HEADS = 16
KEY_VALUE_HEADS = 8
HEAD_SIZE = 64


norm_eps = 1e-06
branch_scale = 0.22
score_scale = 0.015625
rope_base = 10000.0
masked_score = -1e30


def from_behind(array, axis, by):
    count = lax.axis_size(axis)
    pairs = [(i, i + by) for i in range(count) if 0 <= i + by < count]
    return lax.ppermute(array, axis, pairs)


def shortened(array):
    return jax.tree.map(lambda a: a.astype(jnp.bfloat16) if a.dtype == jnp.float32 else a, array)


def norm_rows(vectors, gain_vec):
    inverse = lax.rsqrt(jnp.mean(vectors * vectors, axis=-1, keepdims=True) + norm_eps)
    normed = vectors * inverse
    return (normed * gain_vec, normed, inverse)


def norm_back(upstream, normed, inverse, gain_vec):
    scaled_grad = upstream * gain_vec
    gain_grad = jnp.sum(upstream * normed, axis=0)
    inner_mean = jnp.mean(scaled_grad * normed, axis=-1, keepdims=True)
    return (inverse * (scaled_grad - normed * inner_mean), gain_grad)


def rope_tables(permitted_mask):
    offsets = (jnp.sum(permitted_mask.astype(jnp.int32), axis=1) - 1).astype(jnp.float32)
    half_dim = HEAD_SIZE // 2
    frequency = rope_base ** (-(jnp.arange(half_dim, dtype=jnp.float32) * 2.0 / HEAD_SIZE))
    angles = offsets[:, None] * frequency[None, :]
    return (jnp.cos(angles)[:, None, :], jnp.sin(angles)[:, None, :])


def rotate(vectors, cosine, sine):
    half_dim = vectors.shape[-1] // 2
    front_half = vectors[..., :half_dim]
    back_half = vectors[..., half_dim:]
    return jnp.concatenate(
        [front_half * cosine - back_half * sine, back_half * cosine + front_half * sine], axis=-1
    )


def rotate_back(vectors, cosine, sine):
    half_dim = vectors.shape[-1] // 2
    front_half = vectors[..., :half_dim]
    back_half = vectors[..., half_dim:]
    return jnp.concatenate(
        [front_half * cosine + back_half * sine, back_half * cosine - front_half * sine], axis=-1
    )


def allowed_pairs(segment):
    position = jnp.arange(segment.shape[0], dtype=jnp.int32)
    return (segment[:, None] == segment[None, :]) & (position[None, :] <= position[:, None])


def attend(query_rows, key_matrix, value_matrix, permitted_mask):
    scores = (
        jnp.einsum("qhgd,khd->hgqk", query_rows, key_matrix, preferred_element_type=jnp.float32)
        * score_scale
    )
    scores = jnp.where(permitted_mask[None, None], scores, masked_score)
    row_max = jnp.max(scores, axis=-1, keepdims=True)
    log_sum_exp = row_max + jnp.log(jnp.sum(jnp.exp(scores - row_max), axis=-1, keepdims=True))
    weights_low = jnp.exp(scores - log_sum_exp).astype(jnp.bfloat16)
    attended = jnp.einsum(
        "hgqk,khd->qhgd", weights_low, value_matrix, preferred_element_type=jnp.float32
    )
    return (attended.astype(jnp.bfloat16), log_sum_exp)


def attention_backward(
    query_rows, key_matrix, value_matrix, permitted_mask, log_sum_exp, head_gradient
):
    scores = (
        jnp.einsum("qhgd,khd->hgqk", query_rows, key_matrix, preferred_element_type=jnp.float32)
        * score_scale
    )
    scores = jnp.where(permitted_mask[None, None], scores, masked_score)
    weights_full = jnp.exp(scores - log_sum_exp)
    weights_low = weights_full.astype(jnp.bfloat16)
    value_gradient = jnp.einsum(
        "hgqk,qhgd->khd", weights_low, head_gradient, preferred_element_type=jnp.float32
    )
    weight_grad = jnp.einsum(
        "qhgd,khd->hgqk", head_gradient, value_matrix, preferred_element_type=jnp.float32
    )
    inner_sum = jnp.sum(weights_full * weight_grad, axis=-1, keepdims=True)
    score_grad = (weights_full * (weight_grad - inner_sum) * score_scale).astype(jnp.bfloat16)
    query_gradient = jnp.einsum(
        "hgqk,khd->qhgd", score_grad, key_matrix, preferred_element_type=jnp.float32
    )
    key_gradient = jnp.einsum(
        "hgqk,qhgd->khd", score_grad, query_rows, preferred_element_type=jnp.float32
    )
    return (query_gradient, key_gradient, value_gradient)


GROUP = ("fsdp", "tp")


def exchange(blocks):
    return lax.all_to_all(blocks, "fsdp", split_axis=0, concat_axis=0, tiled=True)


def expert_matrices(w_gate, w_up, w_down):
    count = lax.axis_size("fsdp")
    experts, depth, hidden_units = w_gate.shape
    local = experts // count
    pair = jnp.stack([w_gate, w_up], axis=0).reshape(2, count, local, depth, hidden_units)
    pair = exchange(pair.transpose(1, 3, 0, 2, 4).reshape(count, depth, -1))
    gate_up = pair.reshape(count * depth, 2 * local * hidden_units)
    down = exchange(w_down.reshape(count, local, w_down.shape[1], w_down.shape[2]))
    down = down.transpose(1, 0, 2, 3).reshape(local * hidden_units, w_down.shape[2])
    return (gate_up, down)


def expert_shards(both_w, down_w, local, hidden_units):
    count = lax.axis_size("fsdp")
    both = exchange(both_w.reshape(count, -1, both_w.shape[1]))
    depth = both.shape[1]
    both = both.reshape(count, depth, 2, local, hidden_units).transpose(2, 0, 3, 1, 4)
    both = both.reshape(2, count * local, depth, hidden_units).astype(jnp.float32)
    down = down_w.reshape(local, count, hidden_units // count, -1).transpose(1, 0, 2, 3)
    down = exchange(down).reshape(count * local, hidden_units // count, -1).astype(jnp.float32)
    return (both[0], both[1], down)


def spread(shares, hidden_units):
    rows, local = shares.shape
    wide = jnp.broadcast_to(shares[:, :, None], (rows, local, hidden_units))
    return wide.reshape(rows, local * hidden_units)


def forward_layer(layer_in, segment, chosen, weights, own):
    w_qkv, w_output, w_router, gain_attn, gain_moe, gate_up, w_down = weights
    first, local = own
    query_width = w_output.shape[0]
    key_width = (w_qkv.shape[1] - query_width) // 2
    key_value_heads = key_width // HEAD_SIZE
    hidden_units = w_down.shape[0] // local
    residual = layer_in.astype(jnp.float32)
    scaled_one, normed_one, inverse_one = norm_rows(residual, gain_attn)
    attn_in = lax.all_gather(scaled_one.astype(jnp.bfloat16), "tp", axis=0, tiled=True)
    count_of_tokens = attn_in.shape[0]
    permitted_mask = allowed_pairs(segment)
    cosine, sine = rope_tables(permitted_mask)
    qkv = jnp.dot(attn_in, w_qkv, preferred_element_type=jnp.float32)
    turned = rotate(
        qkv[:, : query_width + key_width].reshape(count_of_tokens, -1, HEAD_SIZE), cosine, sine
    ).astype(jnp.bfloat16)
    query_rows = turned[:, : query_width // HEAD_SIZE].reshape(
        count_of_tokens, key_value_heads, QUERY_HEADS // KEY_VALUE_HEADS, HEAD_SIZE
    )
    key_matrix = turned[:, query_width // HEAD_SIZE :]
    value_matrix = (
        qkv[:, query_width + key_width :]
        .astype(jnp.bfloat16)
        .reshape(count_of_tokens, key_value_heads, HEAD_SIZE)
    )
    attended, log_sum_exp = attend(query_rows, key_matrix, value_matrix, permitted_mask)
    mixed_heads = attended.reshape(count_of_tokens, -1)
    attn_out = lax.psum_scatter(
        jnp.dot(mixed_heads, w_output, preferred_element_type=jnp.float32).astype(jnp.bfloat16),
        "tp",
        scatter_dimension=0,
        tiled=True,
    ).astype(jnp.float32)
    hidden_state = residual + branch_scale * attn_out
    scaled_two, normed_two, inverse_two = norm_rows(hidden_state, gain_moe)
    own_rows = scaled_two.astype(jnp.bfloat16)
    moe_in = lax.all_gather(own_rows, GROUP, axis=0, tiled=True)
    logits = jnp.dot(moe_in, w_router, preferred_element_type=jnp.float32)
    logits = jnp.where(chosen, logits, masked_score)
    share = jax.nn.softmax(logits, axis=-1)
    share = jnp.where(chosen, share, 0.0)
    slot_share = lax.dynamic_slice_in_dim(share, first, local, 1)
    both_pre = jnp.dot(moe_in, gate_up, preferred_element_type=jnp.float32)
    half = both_pre.shape[1] // 2
    gate_pre = both_pre[:, :half]
    up_pre = both_pre[:, half:]
    hidden = gate_pre * jax.nn.sigmoid(gate_pre) * up_pre
    weighted = (spread(slot_share, hidden_units) * hidden).astype(jnp.bfloat16)
    combined = jnp.dot(weighted, w_down, preferred_element_type=jnp.float32)
    moe_out = lax.psum_scatter(
        combined.astype(jnp.bfloat16), GROUP, scatter_dimension=0, tiled=True
    ).astype(jnp.float32)
    result = (hidden_state + branch_scale * moe_out).astype(jnp.bfloat16)
    kept_state = (
        attn_in,
        query_rows,
        key_matrix,
        value_matrix,
        attended,
        log_sum_exp,
        normed_one,
        inverse_one,
        normed_two,
        inverse_two,
        own_rows,
        moe_in,
        share,
        slot_share,
        both_pre,
        weighted,
        cosine,
        sine,
        permitted_mask,
    )
    return (result, kept_state)


def backward_layer(upstream, kept_state, weights, own):
    w_qkv, w_output, w_router, gain_attn, gain_moe, gate_up, w_down = weights
    first, local = own
    (
        attn_in,
        query_rows,
        key_matrix,
        value_matrix,
        attended,
        log_sum_exp,
        normed_one,
        inverse_one,
        normed_two,
        inverse_two,
        own_rows,
        moe_in,
        share,
        slot_share,
        both_pre,
        weighted,
        cosine,
        sine,
        permitted_mask,
    ) = kept_state
    local_rows = upstream.shape[0]
    count_of_tokens = attn_in.shape[0]
    key_value_heads = key_matrix.shape[1]
    hidden_units = w_down.shape[0] // local
    place = lax.axis_index("fsdp") * lax.axis_size("tp") + lax.axis_index("tp")
    moe_grad = lax.all_gather(
        (branch_scale * upstream).astype(jnp.bfloat16), GROUP, axis=0, tiled=True
    )
    hidden_grad = lax.dot_general(
        moe_grad, w_down, (((1,), (1,)), ((), ())), preferred_element_type=jnp.float32
    )
    half = both_pre.shape[1] // 2
    gate_pre = both_pre[:, :half]
    up_pre = both_pre[:, half:]
    sigmoid_gate = jax.nn.sigmoid(gate_pre)
    hidden = gate_pre * sigmoid_gate * up_pre
    share_part = jnp.sum(
        (hidden_grad * hidden).reshape(moe_grad.shape[0], local, hidden_units), axis=-1
    )
    share_wide = lax.dynamic_update_slice_in_dim(jnp.zeros_like(share), share_part, first, 1)
    share_grad = lax.psum_scatter(share_wide, GROUP, scatter_dimension=0, tiled=True)
    scaled_grad = spread(slot_share, hidden_units) * hidden_grad
    gate_grad = (
        scaled_grad * up_pre * sigmoid_gate * (1.0 + gate_pre * (1.0 - sigmoid_gate))
    ).astype(jnp.bfloat16)
    up_grad = (scaled_grad * gate_pre * sigmoid_gate).astype(jnp.bfloat16)
    both_grad = jnp.concatenate([gate_grad, up_grad], axis=-1)
    token_grad = lax.dot_general(
        both_grad, gate_up, (((1,), (1,)), ((), ())), preferred_element_type=jnp.float32
    )
    norm_grad = lax.psum_scatter(
        token_grad.astype(jnp.bfloat16), GROUP, scatter_dimension=0, tiled=True
    ).astype(jnp.float32)
    own_share = lax.dynamic_slice_in_dim(share, place * local_rows, local_rows, 0)
    logit_grad = (
        own_share * (share_grad - jnp.sum(own_share * share_grad, axis=-1, keepdims=True))
    ).astype(jnp.bfloat16)
    norm_grad = norm_grad + jnp.dot(logit_grad, w_router.T, preferred_element_type=jnp.float32)
    back_two, gain_two = norm_back(norm_grad, normed_two, inverse_two, gain_moe)
    state_grad = upstream + back_two
    attn_grad = lax.all_gather(
        (branch_scale * state_grad).astype(jnp.bfloat16), "tp", axis=0, tiled=True
    )
    mixed_heads = attended.reshape(count_of_tokens, -1)
    head_gradient = jnp.dot(attn_grad, w_output.T, preferred_element_type=jnp.float32).astype(
        jnp.bfloat16
    )
    query_gradient, key_gradient, value_gradient = attention_backward(
        query_rows,
        key_matrix,
        value_matrix,
        permitted_mask,
        log_sum_exp,
        head_gradient.reshape(
            count_of_tokens, key_value_heads, QUERY_HEADS // KEY_VALUE_HEADS, HEAD_SIZE
        ),
    )
    turned = jnp.concatenate(
        [query_gradient.reshape(count_of_tokens, -1, HEAD_SIZE), key_gradient], axis=1
    )
    turned = rotate_back(turned, cosine, sine).reshape(count_of_tokens, -1)
    qkv_grad = jnp.concatenate(
        [turned, value_gradient.reshape(count_of_tokens, -1)], axis=1
    ).astype(jnp.bfloat16)
    input_part = lax.dot_general(
        qkv_grad, w_qkv, (((1,), (1,)), ((), ())), preferred_element_type=jnp.float32
    )
    norm_one_grad = lax.psum_scatter(
        input_part.astype(jnp.bfloat16), "tp", scatter_dimension=0, tiled=True
    ).astype(jnp.float32)
    back_one, gain_one = norm_back(norm_one_grad, normed_one, inverse_one, gain_attn)
    terms = (
        (attn_in, qkv_grad),
        (mixed_heads, attn_grad),
        (logit_grad, own_rows),
        (moe_in, both_grad),
        (weighted, moe_grad),
    )
    return (state_grad + back_one, (gain_one, gain_two), terms)


def summed_product(pairs):
    left = jnp.concatenate([pair[0] for pair in pairs], axis=0)
    right = jnp.concatenate([pair[1] for pair in pairs], axis=0)
    return lax.dot_general(
        left, right, (((0,), (0,)), ((), ())), preferred_element_type=jnp.float32
    )


def per_device(
    inputs,
    segment_ids,
    routes,
    w_query,
    key_weight,
    value_weight,
    w_output,
    w_router,
    gain_attn,
    gain_moe,
    w_gate,
    w_up,
    w_down,
    out_grad,
):
    section_count = lax.axis_size("section")
    section_index = lax.axis_index("section")
    fsdp_count = lax.axis_size("fsdp")
    micro_count = inputs.shape[0]
    local_rows = inputs.shape[1]
    model_width = inputs.shape[2]
    depth = w_query.shape[1]
    expert_count = w_router.shape[2]
    local = expert_count // fsdp_count
    hidden_units = w_gate.shape[3]
    query_width = w_query.shape[2]
    key_width = key_weight.shape[2]
    qkv_width = query_width + 2 * key_width
    flat_output = w_output[0].reshape(depth, -1)
    output_width = flat_output.shape[1]
    packed = jnp.concatenate(
        [
            w_query[0],
            key_weight[0],
            value_weight[0],
            flat_output,
            w_router[0],
            gain_attn[0].astype(jnp.bfloat16)[:, None],
            gain_moe[0].astype(jnp.bfloat16)[:, None],
        ],
        axis=1,
    )
    packed = lax.all_gather(packed, "fsdp", axis=0, tiled=True)
    after = qkv_width + output_width
    gate_up, down_full = expert_matrices(w_gate[0], w_up[0], w_down[0])
    weights = (
        packed[:, :qkv_width],
        packed[:, qkv_width:after].reshape(-1, model_width),
        packed[:, after : after + expert_count],
        packed[:, after + expert_count].astype(jnp.float32),
        packed[:, after + expert_count + 1].astype(jnp.float32),
        gate_up,
        down_full,
    )
    expert_ids = jnp.arange(expert_count, dtype=jnp.int32)
    chosen_rows = jnp.any(routes[0][..., None] == expert_ids, axis=2).astype(jnp.bfloat16)
    chosen_rows = lax.all_gather(chosen_rows, "fsdp", axis=1, tiled=True)
    own = (lax.axis_index("fsdp") * local, local)
    segment_rows = segment_ids[:, 0, :]
    tick_count = micro_count + section_count - 1
    outputs = jnp.zeros((micro_count, local_rows, model_width), jnp.bfloat16)
    history = []
    previous = None
    for tick_step in range(tick_count):
        mb_index = tick_step - section_index
        active = (mb_index >= 0) & (mb_index < micro_count)
        mb_pick = jnp.clip(mb_index, 0, micro_count - 1)
        fresh_input = inputs[min(tick_step, micro_count - 1)]
        if previous is None:
            arrived = jnp.zeros_like(fresh_input)
        else:
            arrived = from_behind(previous, "section", 1)
        layer_in = jnp.where(section_index == 0, fresh_input, arrived)
        segment = lax.dynamic_index_in_dim(segment_rows, mb_pick, 0, keepdims=False)
        chosen = lax.dynamic_index_in_dim(chosen_rows, mb_pick, 0, keepdims=False) > 0.5
        result, kept_state = forward_layer(layer_in, segment, chosen, weights, own)
        outputs = jnp.where(
            active, lax.dynamic_update_index_in_dim(outputs, result, mb_pick, 0), outputs
        )
        history.append(kept_state)
        previous = result
    input_grads = jnp.zeros((micro_count, local_rows, model_width), jnp.float32)
    gain_sums = None
    all_terms = []
    previous = None
    for tick_step in range(tick_count):
        mb_index = micro_count + section_count - 2 - tick_step - section_index
        active = (mb_index >= 0) & (mb_index < micro_count)
        mb_pick = jnp.clip(mb_index, 0, micro_count - 1)
        fresh_grad = out_grad[max(micro_count - 1 - tick_step, 0)].astype(jnp.float32)
        if previous is None:
            arrived = jnp.zeros_like(fresh_grad)
        else:
            arrived = from_behind(shortened(previous), "section", -1).astype(previous.dtype)
        upstream = jnp.where(section_index == section_count - 1, fresh_grad, arrived)
        upstream = jnp.where(active, upstream, jnp.zeros_like(upstream))
        grad_out, gains, terms = backward_layer(
            upstream, history[tick_count - 1 - tick_step], weights, own
        )
        input_grads = jnp.where(
            active, lax.dynamic_update_index_in_dim(input_grads, grad_out, mb_pick, 0), input_grads
        )
        gain_sums = gains if gain_sums is None else tuple(a + b for a, b in zip(gain_sums, gains))
        all_terms.append(terms)
        previous = grad_out
    qkv_pairs, output_pairs, router_pairs, both_pairs, down_pairs = zip(*all_terms)
    both_w = summed_product(both_pairs).astype(jnp.bfloat16)
    down_w = summed_product(down_pairs).astype(jnp.bfloat16)
    gate_shard, up_shard, down_shard = expert_shards(both_w, down_w, local, hidden_units)
    small = jnp.concatenate([summed_product(router_pairs), jnp.stack(gain_sums)], axis=0)
    small = lax.psum(small, "tp").T
    packed_grad = jnp.concatenate(
        [
            summed_product(qkv_pairs),
            summed_product(output_pairs).reshape(model_width, -1),
            small,
        ],
        axis=1,
    ).astype(jnp.bfloat16)
    packed_grad = lax.psum_scatter(
        packed_grad, "fsdp", scatter_dimension=0, tiled=True
    ).astype(jnp.float32)
    shard_sums = (
        packed_grad[:, :query_width],
        packed_grad[:, query_width : query_width + key_width],
        packed_grad[:, query_width + key_width : qkv_width],
        packed_grad[:, qkv_width:after].reshape(-1, model_width),
        packed_grad[:, after : after + expert_count],
        packed_grad[:, after + expert_count],
        packed_grad[:, after + expert_count + 1],
        gate_shard,
        up_shard,
        down_shard,
    )
    return (outputs[None], input_grads[None]) + tuple((part[None] for part in shard_sums))


def solution(mesh):
    in_specs = (
        P(None, ("fsdp", "tp"), None),
        P(None, "fsdp", None),
        P("section", None, "fsdp", None),
        P("section", "fsdp", "tp"),
        P("section", "fsdp", "tp"),
        P("section", "fsdp", "tp"),
        P("section", ("tp", "fsdp"), None),
        P("section", "fsdp", None),
        P("section", "fsdp"),
        P("section", "fsdp"),
        P("section", None, "fsdp", "tp"),
        P("section", None, "fsdp", "tp"),
        P("section", None, ("tp", "fsdp"), None),
        P(None, ("fsdp", "tp"), None),
    )
    out_specs = (
        P("section", None, ("fsdp", "tp"), None),
        P("section", None, ("fsdp", "tp"), None),
        P("section", "fsdp", "tp"),
        P("section", "fsdp", "tp"),
        P("section", "fsdp", "tp"),
        P("section", ("tp", "fsdp"), None),
        P("section", "fsdp", None),
        P("section", "fsdp"),
        P("section", "fsdp"),
        P("section", None, "fsdp", "tp"),
        P("section", None, "fsdp", "tp"),
        P("section", None, ("tp", "fsdp"), None),
    )
    return jax.shard_map(
        per_device, mesh=mesh, in_specs=in_specs, out_specs=out_specs, check_vma=False
    )
```

time: 2090 us -> 1480 us (0.71)
  local copies, waits for them, and re-layouts: 469 us -> 86.9 us
  other arithmetic: 160 us -> 67.7 us
  blocking collectives: 221 us -> 138 us
  waiting for transfers between devices: 991 us -> 916 us
  starting transfers between devices: 10.9 us -> 34 us
    gather x26 -> x0, local copies, waits for them, and re-layouts: 230 us -> none  [the longest x4 72.8 us: dispatch(): picked = jnp.take(rows_in, source, axis=0)]
    reduce_scatter x14 -> x7, waiting for transfers between devices: 585 us -> 405 us  [the longest x3 195 us: forward_layer(): lax.psum_scatter(combined.astype(jnp.bfloat16), GROUP, scatter_dimension=...]
    unnamed x23 -> x26, waiting for transfers between devices: 2.58 us -> 138 us
    all_gather x3 -> x7, waiting for transfers between devices: 344 us -> 248 us  [the longest x3 107 us: backward_layer(): lax.all_gather((branch_scale * upstream).astype(jnp.bfloat16), GROUP, axi...]
    scatter x9 -> x0, local copies, waits for them, and re-layouts: 75.5 us -> none  [the longest x3 25.4 us: route_tables(): jnp.zeros((E * CAP,), jnp.int32).at[slot_index].set(jnp.ones_like(owners))]
    reduce_scatter x3, waiting for transfers between devices: 0.01 us -> 69.3 us  [forward_layer(): lax.psum_scatter(jnp.dot(mixed_heads, w_output, preferred_element_type=jn...]
    dynamic_update_slice x12 -> x3, local copies, waits for them, and re-layouts: 63.4 us -> 2.15 us  [backward_layer(): lax.dynamic_update_slice_in_dim(jnp.zeros_like(share), share_part, first, 1)]
    all_gather x16 -> x4, blocking collectives: 161 us -> 104 us  [the longest x1 83 us: per_device(): chosen_rows = lax.all_gather(chosen_rows, 'fsdp', axis=1, tiled=True)]
  transfers between devices with their start and end apart: 27 -> 31, of which waited for: 15 -> 25; matrix products, arithmetic and copies ran while one was open for 18% -> 12% of each run, Pallas kernels for 0% -> 0%
where the time goes in v1:
time: 1480 us; the launch traced here: 1470 us
  waiting for transfers between devices  916 us (62%)
  matrix products  210 us (14%)
  blocking collectives  138 us (9%)
  local copies, waits for them, and re-layouts  86.9 us (6%)
  other arithmetic  67.7 us (5%)
  starting transfers between devices  34 us (2%)
  between operations  16.4 us (1%)
    reduce_scatter x3, waiting for transfers between devices, forward_layer(): lax.psum_scatter(combined.astype(jnp.bfloat16), GROUP, scatter_dimension=...  195 us
    reduce_scatter x3, waiting for transfers between devices, backward_layer(): lax.psum_scatter(token_grad.astype(jnp.bfloat16), GROUP, scatter_dimensio...  186 us
    unnamed x26, waiting for transfers between devices  138 us
    all_gather x3, waiting for transfers between devices, backward_layer(): lax.all_gather((branch_scale * upstream).astype(jnp.bfloat16), GROUP, axi...  107 us
    all_gather x1, blocking collectives, per_device(): chosen_rows = lax.all_gather(chosen_rows, 'fsdp', axis=1, tiled=True)  83 us
    all_gather x3, waiting for transfers between devices, forward_layer(): moe_in = lax.all_gather(own_rows, GROUP, axis=0, tiled=True)  81.6 us
    reduce_scatter x3, waiting for transfers between devices, forward_layer(): lax.psum_scatter(jnp.dot(mixed_heads, w_output, preferred_element_type=jn...  69.3 us
    all_gather x1, waiting for transfers between devices, per_device(): packed = lax.all_gather(packed, 'fsdp', axis=0, tiled=True)  59.3 us
  transfers between devices with their start and end apart: 31, of which 25 were waited for; matrix products, arithmetic and copies ran while one was open for 12% of the time, Pallas kernels for 0%

profile of v1, /device:TPU:0, one launch (start us, length us, event | category | flops | bytes accessed | tf_op | source)
XLA Modules:
  0.0 1469.1 jit_solution(12295021851691268621)
XLA Ops:
  12.7 6.4 all-to-all-start.1
  23.2 6.3 copy.196
  31.1 59.3 %all-gather.8.cloned.1.call-done = bf16[1024,802]{1,0:T(8,128)(2,1)} async-done(((bf16[256,802]{1,0:T(8,128)(2,1)}), bf16[1024,802]{1,0:T(8,128)(2,1)}) %all-gather.8.cloned.1.call-update) | async-done | bytes 1642512 | tf_op jit(solution)/shard_map/all_gather | solution.py:384
  92.0 7.2 all_gather.43
  103.2 6.4 all-to-all-start
  111.0 25.2 %reduce-scatter.23.cloned.1.call-done = bf16[64,1024]{1,0:T(8,128)(2,1)} async-done(((bf16[256,1024]{1,0:T(8,128)(2,1)}), bf16[64,1024]{1,0:T(8,128)(2,1)}) %reduce-scatter.23.cloned.1.call-update) | async-done | bytes 131088 | tf_op jit(solution)/shard_map/reduce_scatter | solution.py:178
  139.2 83.0 %all_gather.44 = bf16[2,1024,32]{1,2,0:T(8,128)(2,1)S(1)} all-gather(bf16[2,256,32]{1,2,0:T(8,128)(2,1)S(1)} %convert_element_type.373), channel_id=1, replica_groups=mesh['section'=2,'fsdp'=4,'tp'=4] {'fsdp'}, dimensions={1}, use_global_device_ids=true | all-gather | bytes 163840 | tf_op jit(solution)/shard_map/all_gather | solution.py:398
  225.4 6.3 copy.197
  234.4 6.9 fusion.288
  251.2 61.7 %reduce-scatter.25.cloned.1.call-done = bf16[64,1024]{1,0:T(8,128)(2,1)} async-done(((bf16[1024,1024]{1,0:T(8,128)(2,1)}), bf16[64,1024]{1,0:T(8,128)(2,1)}) %reduce-scatter.25.cloned.1.call-update) | async-done | bytes 131088 | tf_op jit(solution)/shard_map/reduce_scatter | solution.py:200
  320.1 6.7 all_gather.46
  334.2 22.0 %reduce-scatter.27.cloned.1.call-done = bf16[64,1024]{1,0:T(8,128)(2,1)} async-done(((bf16[256,1024]{1,0:T(8,128)(2,1)}), bf16[64,1024]{1,0:T(8,128)(2,1)}) %reduce-scatter.27.cloned.1.call-update) | async-done | bytes 131088 | tf_op jit(solution)/shard_map/reduce_scatter | solution.py:178
  359.3 41.3 %all-gather.12.cloned.1.call-done = bf16[1024,1024]{1,0:T(8,128)(2,1)} async-done(((bf16[64,1024]{1,0:T(8,128)(2,1)}), bf16[1024,1024]{1,0:T(8,128)(2,1)}) %all-gather.12.cloned.1.call-update) | async-done | bytes 2097168 | tf_op jit(solution)/shard_map/all_gather | solution.py:187
  403.9 6.9 fusion.289
  420.8 60.6 %reduce-scatter.29.cloned.1.call-done = bf16[64,1024]{1,0:T(8,128)(2,1)} async-done(((bf16[1024,1024]{1,0:T(8,128)(2,1)}), bf16[64,1024]{1,0:T(8,128)(2,1)}) %reduce-scatter.29.cloned.1.call-update) | async-done | bytes 131088 | tf_op jit(solution)/shard_map/reduce_scatter | solution.py:200
  488.6 6.7 all_gather.48
  506.0 22.1 %reduce-scatter.31.cloned.1.call-done = bf16[64,1024]{1,0:T(8,128)(2,1)} async-done(((bf16[256,1024]{1,0:T(8,128)(2,1)}), bf16[64,1024]{1,0:T(8,128)(2,1)}) %reduce-scatter.31.cloned.1.call-update) | async-done | bytes 131088 | tf_op jit(solution)/shard_map/reduce_scatter | solution.py:178
  532.7 40.3 %all-gather.14.cloned.1.call-done = bf16[1024,1024]{1,0:T(8,128)(2,1)} async-done(((bf16[64,1024]{1,0:T(8,128)(2,1)}), bf16[1024,1024]{1,0:T(8,128)(2,1)}) %all-gather.14.cloned.1.call-update) | async-done | bytes 2097168 | tf_op jit(solution)/shard_map/all_gather | solution.py:187
  579.4 10.7 fusion.290
  590.0 25.7 %all-gather.16.cloned.1.call-done = bf16[1024,1024]{1,0:T(8,128)(2,1)} async-done(((bf16[64,1024]{1,0:T(8,128)(2,1)}), bf16[1024,1024]{1,0:T(8,128)(2,1)}) %all-gather.16.cloned.1.call-update) | async-done | bytes 2097168 | tf_op jit(solution)/shard_map/all_gather | solution.py:257
  618.1 8.7 multiply_convert_fusion.5
  640.1 9.3 fusion.62
  649.4 45.4 %reduce-scatter.49.cloned.1.call-done = f32[64,32]{1,0:T(8,128)} async-done(((f32[1024,32]{1,0:T(8,128)}), f32[64,32]{1,0:T(8,128)}) %reduce-scatter.49.cloned.1.call-update) | async-done | bytes 8208
  698.5 61.4 %reduce-scatter.35.cloned.1.call-done = bf16[64,1024]{1,0:T(8,128)(2,1)} async-done(((bf16[1024,1024]{1,0:T(8,128)(2,1)}), bf16[64,1024]{1,0:T(8,128)(2,1)}) %reduce-scatter.35.cloned.1.call-update) | async-done | bytes 131088 | tf_op jit(solution)/shard_map/reduce_scatter | solution.py:282
  763.6 6.7 all_gather.51
  785.2 21.1 %reduce-scatter.37.cloned.1.call-done = bf16[64,1024]{1,0:T(8,128)(2,1)} async-done(((bf16[256,1024]{1,0:T(8,128)(2,1)}), bf16[64,1024]{1,0:T(8,128)(2,1)}) %reduce-scatter.37.cloned.1.call-update) | async-done | bytes 131088 | tf_op jit(solution)/shard_map/reduce_scatter | solution.py:319
  809.8 5.7 collective-permute-done.2
  816.4 40.4 %all-gather.18.cloned.1.call-done = bf16[1024,1024]{1,0:T(8,128)(2,1)} async-done(((bf16[64,1024]{1,0:T(8,128)(2,1)}), bf16[1024,1024]{1,0:T(8,128)(2,1)}) %all-gather.18.cloned.1.call-update) | async-done | bytes 2097168 | tf_op jit(solution)/shard_map/all_gather | solution.py:257
  856.9 12.0 multiply_convert_fusion.3
  878.0 9.3 fusion.59
  887.4 45.5 %reduce-scatter.51.cloned.1.call-done = f32[64,32]{1,0:T(8,128)} async-done(((f32[1024,32]{1,0:T(8,128)}), f32[64,32]{1,0:T(8,128)}) %reduce-scatter.51.cloned.1.call-update) | async-done | bytes 8208
  935.4 62.6 %reduce-scatter.39.cloned.1.call-done = bf16[64,1024]{1,0:T(8,128)(2,1)} async-done(((bf16[1024,1024]{1,0:T(8,128)(2,1)}), bf16[64,1024]{1,0:T(8,128)(2,1)}) %reduce-scatter.39.cloned.1.call-update) | async-done | bytes 131088 | tf_op jit(solution)/shard_map/reduce_scatter | solution.py:282
  999.9 7.1 all_gather.53
  1021.7 21.1 %reduce-scatter.41.cloned.1.call-done = bf16[64,1024]{1,0:T(8,128)(2,1)} async-done(((bf16[256,1024]{1,0:T(8,128)(2,1)}), bf16[64,1024]{1,0:T(8,128)(2,1)}) %reduce-scatter.41.cloned.1.call-update) | async-done | bytes 131088 | tf_op jit(solution)/shard_map/reduce_scatter | solution.py:319
  1046.7 5.7 collective-permute-done.3
  1053.2 40.6 %all-gather.20.cloned.1.call-done = bf16[1024,1024]{1,0:T(8,128)(2,1)} async-done(((bf16[64,1024]{1,0:T(8,128)(2,1)}), bf16[1024,1024]{1,0:T(8,128)(2,1)}) %all-gather.20.cloned.1.call-update) | async-done | bytes 2097168 | tf_op jit(solution)/shard_map/all_gather | solution.py:257
  1093.8 12.1 multiply_convert_fusion.1
  1113.7 9.3 fusion.56
  1123.1 11.5 fusion.51
  1140.9 46.3 %reduce-scatter.53.cloned.1.call-done = f32[64,32]{1,0:T(8,128)} async-done(((f32[1024,32]{1,0:T(8,128)}), f32[64,32]{1,0:T(8,128)}) %reduce-scatter.53.cloned.1.call-update) | async-done | bytes 8208
  1189.6 61.6 %reduce-scatter.43.cloned.1.call-done = bf16[64,1024]{1,0:T(8,128)(2,1)} async-done(((bf16[1024,1024]{1,0:T(8,128)(2,1)}), bf16[64,1024]{1,0:T(8,128)(2,1)}) %reduce-scatter.43.cloned.1.call-update) | async-done | bytes 131088 | tf_op jit(solution)/shard_map/reduce_scatter | solution.py:282
  1253.9 7.0 all_gather.55
  1270.8 34.6 %fusion.46 = bf16[1024,2048]{1,0:T(8,128)(2,1)} fusion(bf16[1024,1024]{1,0:T(8,128)(2,1)} %get-tuple-element.101, bf16[1024,1024]{1,0:T(8,128)(2,1)} %get-tuple-element.100, bf16[1024,1024]{1,0:T(8,128)(2,1)} %get-tuple-element.103, bf16[1024,1024]{1,0:T(8,128)(2,1)} %get-tuple-element.102, bf16[1024,1024]{1,0:T(8,128)(2,1)} %get-tuple-element.105, ...), kind=kOutput, calls=%fused_computation.69 | convolution fusion | flops 12981370880 | bytes 23068672 | tf_op jit(solution)/shard_map/dot_general | solution.py:336
  1305.4 4.9 all-to-all-start.2
  1310.5 6.1 convolution_convert_fusion
  1326.6 13.4 all-reduce.1
  1342.6 72.9 %reduce-scatter.33.cloned.1.call-done = bf16[64,1024]{1,0:T(8,128)(2,1)} async-done(((bf16[1024,1024]{1,0:T(8,128)(2,1)}), bf16[64,1024]{1,0:T(8,128)(2,1)}) %reduce-scatter.33.cloned.1.call-update) | async-done | bytes 131088 | tf_op jit(solution)/shard_map/reduce_scatter | solution.py:200
  1431.6 24.0 %reduce-scatter.47.cloned.1.call-done = bf16[256,802]{0,1:T(8,128)(2,1)} async-done(((bf16[1024,802]{0,1:T(8,128)(2,1)}), bf16[256,802]{0,1:T(8,128)(2,1)}) %reduce-scatter.47.cloned.1.call-update) | async-done | bytes 410640 | tf_op jit(solution)/shard_map/reduce_scatter | solution.py:461
  (479 shorter events, 234.6 us)
Async XLA Ops:
  7.2 83.2 %all-gather.8.cloned.1.call-start = ((), (), s32[]{:S(2)}) async-start(), calls=%async_computation.20 | async-start | bytes 2293760 | tf_op jit(solution)/shard_map/all_gather | solution.py:384
  12.7 90.3 %all-to-all-start.1 = ((bf16[4,8,32,1024]{3,2,1,0:T(8,128)(2,1)}), bf16[4,8,32,1024]{3,2,1,0:T(8,128)(2,1)}, u32[]{:S(2)}, u32[]{:S(2)}) async-start(bf16[4,8,32,1024]{3,2,1,0:T(8,128)(2,1)} %bitcast.396), calls=%async_computation.2 | async-start | bytes 4194304 | tf_op jit(solution)/shard_map/all_to_all | solution.py:118
  31.1 299.1 %copy-start.66 = (f32[256,32]{0,1:T(8,128)}, f32[256,32]{0,1:T(8,128)S(1)}, u32[]{:S(2)}) copy-start(f32[256,32]{0,1:T(8,128)S(1)} %get-tuple-element.137) | copy-start | bytes 98308
  31.1 299.1 %copy-start.67 = (f32[256,32]{0,1:T(8,128)}, f32[256,32]{0,1:T(8,128)S(1)}, u32[]{:S(2)}) copy-start(f32[256,32]{0,1:T(8,128)S(1)} %get-tuple-element.138) | copy-start | bytes 98308
  103.2 122.2 %all-to-all-start = ((bf16[4,256,2048]{1,2,0:T(8,128)(2,1)}), bf16[4,256,2048]{1,2,0:T(8,128)(2,1)}, u32[]{:S(2)}, u32[]{:S(2)}) async-start(bf16[4,256,2048]{1,2,0:T(8,128)(2,1)} %bitcast.378), calls=%async_computation.1 | async-start | bytes 8388608 | tf_op jit(solution)/shard_map/all_to_all | solution.py:118
  109.5 26.7 %reduce-scatter.23.cloned.1.call-start = ((), (), s32[]{:S(2)}) async-start(), calls=%async_computation.21 | async-start | bytes 655360 | tf_op jit(solution)/shard_map/reduce_scatter | solution.py:178
  109.8 121.9 %copy-start.42 = (bf16[2,64,2,256]{3,1,2,0:T(8,128)(2,1)}, bf16[2,64,2,256]{3,1,2,0:T(8,128)(2,1)S(1)}, u32[]{:S(2)}) copy-start(bf16[2,64,2,256]{3,1,2,0:T(8,128)(2,1)S(1)} %convolution_convert_fusion.14) | copy-start | bytes 393220
  111.0 120.7 %all-gather.10.cloned.1.call-start = ((), (), s32[]{:S(2)}) async-start(), calls=%async_computation.22 | async-start | bytes 2228224 | tf_op jit(solution)/shard_map/all_gather | solution.py:187
  139.0 173.9 %reduce-scatter.25.cloned.1.call-start = ((), (), s32[]{:S(2)}) async-start(), calls=%async_computation.23 | async-start | bytes 2228224 | tf_op jit(solution)/shard_map/reduce_scatter | solution.py:200
  222.2 180.8 %copy-start.20 = (bf16[2,1024,32]{1,2,0:T(8,128)(2,1)}, bf16[2,1024,32]{1,2,0:T(8,128)(2,1)S(1)}, u32[]{:S(2)}) copy-start(bf16[2,1024,32]{1,2,0:T(8,128)(2,1)S(1)} %all_gather.44) | copy-start | bytes 393220
  251.1 105.1 %reduce-scatter.27.cloned.1.call-start = ((), (), s32[]{:S(2)}) async-start(), calls=%async_computation.24 | async-start | bytes 655360 | tf_op jit(solution)/shard_map/reduce_scatter | solution.py:178
  314.0 5.9 collective-permute-start
  334.2 66.4 %all-gather.12.cloned.1.call-start = ((), (), s32[]{:S(2)}) async-start(), calls=%async_computation.25 | async-start | bytes 2228224 | tf_op jit(solution)/shard_map/all_gather | solution.py:187
  359.0 122.4 %reduce-scatter.29.cloned.1.call-start = ((), (), s32[]{:S(2)}) async-start(), calls=%async_computation.26 | async-start | bytes 2228224 | tf_op jit(solution)/shard_map/reduce_scatter | solution.py:200
  420.7 107.4 %reduce-scatter.31.cloned.1.call-start = ((), (), s32[]{:S(2)}) async-start(), calls=%async_computation.27 | async-start | bytes 655360 | tf_op jit(solution)/shard_map/reduce_scatter | solution.py:178
  482.4 5.9 collective-permute-start.1
  506.0 67.0 %all-gather.14.cloned.1.call-start = ((), (), s32[]{:S(2)}) async-start(), calls=%async_computation.28 | async-start | bytes 2228224 | tf_op jit(solution)/shard_map/all_gather | solution.py:187
  531.4 84.4 %all-gather.16.cloned.1.call-start = ((), (), s32[]{:S(2)}) async-start(), calls=%async_computation.30 | async-start | bytes 2228224 | tf_op jit(solution)/shard_map/all_gather | solution.py:257
  532.2 162.7 %reduce-scatter.49.cloned.1.call-start = ((), (), s32[]{:S(2)}) async-start(), calls=%async_computation.40 | async-start | bytes 557056
  639.8 120.1 %reduce-scatter.35.cloned.1.call-start = ((), (), s32[]{:S(2)}) async-start(), calls=%async_computation.31 | async-start | bytes 2228224 | tf_op jit(solution)/shard_map/reduce_scatter | solution.py:282
  649.4 156.9 %reduce-scatter.37.cloned.1.call-start = ((), (), s32[]{:S(2)}) async-start(), calls=%async_computation.32 | async-start | bytes 655360 | tf_op jit(solution)/shard_map/reduce_scatter | solution.py:319
  785.1 71.8 %all-gather.18.cloned.1.call-start = ((), (), s32[]{:S(2)}) async-start(), calls=%async_computation.33 | async-start | bytes 2228224 | tf_op jit(solution)/shard_map/all_gather | solution.py:257
  808.5 7.0 collective-permute-start.2
  816.2 116.7 %reduce-scatter.51.cloned.1.call-start = ((), (), s32[]{:S(2)}) async-start(), calls=%async_computation.41 | async-start | bytes 557056
  877.9 120.0 %reduce-scatter.39.cloned.1.call-start = ((), (), s32[]{:S(2)}) async-start(), calls=%async_computation.34 | async-start | bytes 2228224 | tf_op jit(solution)/shard_map/reduce_scatter | solution.py:282
  877.9 120.0 %copy-start.26 = (bf16[64,1024]{1,0:T(8,128)(2,1)S(1)}, bf16[64,1024]{1,0:T(8,128)(2,1)}, u32[]{:S(2)}) copy-start(bf16[64,1024]{1,0:T(8,128)(2,1)} %reduce-scatter.27.cloned.1.call-done) | copy-start | bytes 393220
  878.0 120.0 %copy-start.101 = (f32[64]{0:T(128)S(1)}, f32[64]{0:T(128)}, u32[]{:S(2)}) copy-start(f32[64]{0:T(128)} %copy-done.100) | copy-start | bytes 772
  887.3 155.4 %reduce-scatter.41.cloned.1.call-start = ((), (), s32[]{:S(2)}) async-start(), calls=%async_computation.35 | async-start | bytes 655360 | tf_op jit(solution)/shard_map/reduce_scatter | solution.py:319
  1021.6 72.2 %all-gather.20.cloned.1.call-start = ((), (), s32[]{:S(2)}) async-start(), calls=%async_computation.36 | async-start | bytes 2228224 | tf_op jit(solution)/shard_map/all_gather | solution.py:257
  1045.4 7.0 collective-permute-start.3
  1053.1 134.0 %reduce-scatter.53.cloned.1.call-start = ((), (), s32[]{:S(2)}) async-start(), calls=%async_computation.42 | async-start | bytes 557056
  1113.5 137.6 %reduce-scatter.43.cloned.1.call-start = ((), (), s32[]{:S(2)}) async-start(), calls=%async_computation.37 | async-start | bytes 2228224 | tf_op jit(solution)/shard_map/reduce_scatter | solution.py:282
  1134.6 116.5 %copy-start.97 = (f32[64]{0:T(128)S(1)}, f32[64]{0:T(128)}, u32[]{:S(2)}) copy-start(f32[64]{0:T(128)} %copy-done.96) | copy-start | bytes 772
  1134.6 118.4 %copy-start.49 = (bf16[64,1024]{1,0:T(8,128)(2,1)S(1)}, bf16[64,1024]{1,0:T(8,128)(2,1)}, u32[]{:S(2)}) copy-start(bf16[64,1024]{1,0:T(8,128)(2,1)} %copy-done.48) | copy-start | bytes 393220
  1136.2 127.2 %copy-start.3 = (f32[2,2,256,256]{2,3,1,0:T(8,128)S(1)}, f32[2,2,256,256]{2,3,1,0:T(8,128)}, u32[]{:S(2)}) copy-start(f32[2,2,256,256]{2,3,1,0:T(8,128)} %copy-done.2) | copy-start | bytes 3145732
  1136.2 127.2 %copy-start.80 = (f32[2,2,256]{2,1,0:T(2,128)S(1)}, f32[2,2,256]{2,1,0:T(2,128)}, u32[]{:S(2)}) copy-start(f32[2,2,256]{2,1,0:T(2,128)} %copy-done.79) | copy-start | bytes 12292
  1136.2 169.2 %all-to-all-start.3 = ((bf16[4,8,32,1024]{3,2,1,0:T(8,128)(2,1)}), bf16[4,8,32,1024]{3,2,1,0:T(8,128)(2,1)}, u32[]{:S(2)}, u32[]{:S(2)}) async-start(bf16[4,8,32,1024]{3,2,1,0:T(8,128)(2,1)} %bitcast.383), calls=%async_computation.16 | async-start | bytes 4194304 | tf_op jit(solution)/shard_map/all_to_all | solution.py:118
  1140.8 184.4 %reduce-scatter.45.cloned.1.call-start = ((), (), s32[]{:S(2)}) async-start(), calls=%async_computation.38 | async-start | bytes 655360 | tf_op jit(solution)/shard_map/reduce_scatter | solution.py:319
  1305.4 115.9 %all-to-all-start.2 = ((bf16[4,256,2048]{2,1,0:T(8,128)(2,1)}), bf16[4,256,2048]{2,1,0:T(8,128)(2,1)}, u32[]{:S(2)}, u32[]{:S(2)}) async-start(bf16[4,256,2048]{2,1,0:T(8,128)(2,1)} %bitcast.392), calls=%async_computation.15 | async-start | bytes 8388608 | tf_op jit(solution)/shard_map/all_to_all | solution.py:118
  1310.4 105.1 %reduce-scatter.33.cloned.1.call-start = ((), (), s32[]{:S(2)}) async-start(), calls=%async_computation.29 | async-start | bytes 2228224 | tf_op jit(solution)/shard_map/reduce_scatter | solution.py:200
  1316.6 139.0 %reduce-scatter.47.cloned.1.call-start = ((), (), s32[]{:S(2)}) async-start(), calls=%async_computation.39 | async-start | bytes 2068480 | tf_op jit(solution)/shard_map/reduce_scatter | solution.py:461
  1325.1 90.4 %copy-start.27 = (bf16[64,1024]{1,0:T(8,128)(2,1)S(1)}, bf16[64,1024]{1,0:T(8,128)(2,1)}, u32[]{:S(2)}) copy-start(bf16[64,1024]{1,0:T(8,128)(2,1)} %reduce-scatter.31.cloned.1.call-done) | copy-start | bytes 393220
  1325.1 91.4 %copy-start.31 = (bf16[64,1024]{1,0:T(8,128)(2,1)S(1)}, bf16[64,1024]{1,0:T(8,128)(2,1)}, u32[]{:S(2)}) copy-start(bf16[64,1024]{1,0:T(8,128)(2,1)} %reduce-scatter.37.cloned.1.call-done) | copy-start | bytes 393220
  1325.1 91.4 %copy-start.86 = (f32[64]{0:T(128)S(1)}, f32[64]{0:T(128)}, u32[]{:S(2)}) copy-start(f32[64]{0:T(128)} %copy-done.85) | copy-start | bytes 772
  1325.2 91.4 %copy-start.99 = (f32[64]{0:T(128)S(1)}, f32[64]{0:T(128)}, u32[]{:S(2)}) copy-start(f32[64]{0:T(128)} %copy-done.98) | copy-start | bytes 772
  1325.2 91.6 %copy-start.32 = (bf16[64,1024]{1,0:T(8,128)(2,1)S(1)}, bf16[64,1024]{1,0:T(8,128)(2,1)}, u32[]{:S(2)}) copy-start(bf16[64,1024]{1,0:T(8,128)(2,1)} %reduce-scatter.41.cloned.1.call-done) | copy-start | bytes 393220
  1325.2 91.6 %copy-start.84 = (f32[64]{0:T(128)S(1)}, f32[64]{0:T(128)}, u32[]{:S(2)}) copy-start(f32[64]{0:T(128)} %copy-done.83) | copy-start | bytes 772
  1325.2 91.6 %copy-start.103 = (f32[64]{0:T(128)S(1)}, f32[64]{0:T(128)}, u32[]{:S(2)}) copy-start(f32[64]{0:T(128)} %copy-done.102) | copy-start | bytes 772
  (90 other events, 1538.4 us)
Sparse Core Ops, SparseCore 0:
  12.9 77.4 all-gather.7
  113.4 22.8 reduce-scatter.22
  139.1 72.0 all-gather.9
  251.3 61.5 reduce-scatter.24
  334.3 21.9 reduce-scatter.26
  359.1 41.4 all-gather.11
  420.8 60.5 reduce-scatter.28
  506.1 21.9 reduce-scatter.30
  531.5 41.4 all-gather.13
  575.5 40.1 all-gather.15
  640.0 54.8 reduce-scatter.48
  699.0 60.8 reduce-scatter.34
  785.2 20.9 reduce-scatter.36
  816.3 40.5 all-gather.17
  878.0 54.8 reduce-scatter.50
  937.1 60.8 reduce-scatter.38
  1021.7 20.9 reduce-scatter.40
  1053.3 40.5 all-gather.19
  1113.6 73.4 reduce-scatter.52
  1191.3 59.8 reduce-scatter.42
  1270.9 20.9 reduce-scatter.44
  1316.7 98.7 reduce-scatter.32
  1417.8 37.7 reduce-scatter.46
